TPU v7x, 32 devices: a whole 2x2x4 slice. The times are simulated.
32 devices in a mesh: cls: 2 (over core), img: 16 (over z, y, x).
Axes of the slice: x: 2, y: 2, z: 4, core: 2. Of those that a mesh axis runs over, the one named last changes fastest.
Arguments:
- images: bfloat16 [1792, 7200], P(('cls', 'img')), may hold values from -8 to 8
- projections: bfloat16 [256, 7200], P('cls'), may hold values from -0.42426407 to 0.42426407
- noise_power: float32 [32, 7200], replicated, may hold values from 0.5 to 4
- class_logprior: float32 [4], replicated, may hold values from -1.5 to 1.5
- groups: int32 [1792], P(('cls', 'img')), may hold values from 0 to 31
- offsets: int32 [1792], P(('cls', 'img')), may hold values from 0 to 3
Outputs:
- weighted_sums: float32 [256, 7200], P(('cls', 'img'))
- log_evidence: float32 [1792], P(('cls', 'img'))
All inputs are finite; a program needn't handle non-finite values.
Results may differ from a plain program's by a relative error of at most 0.0064.
Values may be sent and summed in bfloat16 or wider, within the bound.
No kernel may reach another device: no remote copies, remote signals or barrier semaphores. Data moves between devices by JAX's collectives and lax.ppermute only.
A program may use at most 64 MiB of HBM per device.

v0:
```python
import jax
import jax.numpy as jnp
from jax import lax
from jax.sharding import PartitionSpec as P


def combined_all(value, axis, join):
    pieces = jax.tree.map(lambda part: lax.all_gather(part, axis), value)
    head = jax.tree.map(lambda part: part[0], pieces)
    tail = jax.tree.map(lambda part: part[1:], pieces)
    total, _ = lax.scan(lambda total, section: (join(total, section), None), head, tail)
    return total


def merge_parts(first, second):
    peak = jnp.maximum(first[0], second[0])
    return (peak, first[1] * jnp.exp(first[0] - peak) + second[1] * jnp.exp(second[0] - peak))


def body(images, projections, noise_power, class_logprior, groups, offsets):
    rows_here = images.shape[0]
    proj_here = projections.shape[0]
    cycle_size = lax.axis_size("cls")
    cycle_place = lax.axis_index("cls")
    group_count = noise_power.shape[0]
    class_count = class_logprior.shape[0]
    inverse = 1.0 / noise_power
    group_hot = (groups[:, None] == jnp.arange(group_count, dtype=jnp.int32)[None, :]).astype(
        jnp.float32
    )
    offset_hot = (offsets[:, None] == jnp.arange(class_count, dtype=jnp.int32)[None, :]).astype(
        jnp.float32
    )
    row_inverse = jnp.dot(group_hot, inverse, precision=lax.Precision.HIGHEST)
    whitened = (images.astype(jnp.float32) * row_inverse).astype(jnp.bfloat16)
    tag_rows = jnp.concatenate([group_hot, offset_hot], axis=1).astype(jnp.bfloat16)
    proj_float = projections.astype(jnp.float32)
    quadratic = jnp.dot(inverse, (proj_float * proj_float).T, precision=lax.Precision.HIGHEST)
    global_index = cycle_place * proj_here + jnp.arange(proj_here, dtype=jnp.int32)
    per_class = proj_here * cycle_size // class_count
    class_of = global_index // per_class
    class_shift = (
        class_of[None, :] - jnp.arange(class_count, dtype=jnp.int32)[:, None]
    ) % class_count
    matches = class_shift[:, :, None] == jnp.arange(class_count, dtype=jnp.int32)[None, None, :]
    prior_table = jnp.sum(jnp.where(matches, class_logprior[None, None, :], 0.0), axis=2)
    bias_table = jnp.concatenate([-0.5 * quadratic, prior_table], axis=0)
    gathered, labels = (
        lax.all_gather(whitened, "cls", axis=0, tiled=True),
        lax.all_gather(tag_rows, "cls", axis=0, tiled=True),
    )
    products = jnp.einsum("bf,pf->bp", gathered, projections, preferred_element_type=jnp.float32)
    scores = products + jnp.dot(
        labels.astype(jnp.float32), bias_table, precision=lax.Precision.HIGHEST
    )
    local_peak = jnp.max(scores, axis=1)
    local_sum = jnp.sum(jnp.exp(scores - local_peak[:, None]), axis=1)
    peak, exp_sum = combined_all((local_peak, local_sum), "cls", merge_parts)
    evidence = peak + jnp.log(exp_sum)
    posterior = jnp.exp(scores - evidence[:, None]).astype(jnp.bfloat16)
    sum_rows = lax.psum_scatter(
        jnp.einsum("bp,bf->pf", posterior, gathered, preferred_element_type=jnp.float32),
        "img",
        scatter_dimension=0,
        tiled=True,
    )
    own_evidence = lax.dynamic_slice_in_dim(evidence, cycle_place * rows_here, rows_here)
    return (sum_rows, own_evidence)


def solution(mesh):
    in_specs = (
        P(("cls", "img"), None),
        P("cls", None),
        P(),
        P(),
        P(("cls", "img")),
        P(("cls", "img")),
    )
    out_specs = (P(("cls", "img"), None), P(("cls", "img")))
    return jax.shard_map(body, mesh=mesh, in_specs=in_specs, out_specs=out_specs, check_vma=False)
```

profile of v0, /device:TPU:0, one launch (start us, length us, event | category | flops | bytes accessed | tf_op | source)
XLA Modules:
  0.0 200.8 jit_solution(7838079387105643882)
XLA Ops:
  7.2 0.0 all-gather.5.cloned.1.call-start
  7.3 3.4 %fusion = bf16[56,7200]{1,0:T(8,128)(2,1)} fusion(bf16[56,7200]{1,0:T(8,128)(2,1)} %param.6, f32[32,7200]{1,0:T(8,128)} %param.8, s32[56]{0:T(128)} %param.10), kind=kOutput, calls=%fused_computation.1 | convolution fusion | flops 156270592 | bytes 2534624 | tf_op jit(solution)/shard_map/dot_general | solution.py:34
  10.7 0.0 all-gather.5.cloned.1.call-update
  10.7 0.0 all-reduce.6.cloned.1.call-start
  10.8 2.0 all-gather.2
  12.8 0.1 reshape.106
  12.9 0.6 dynamic-slice
  14.2 0.1 select_reduce_fusion
  14.3 2.3 %fusion.4 = f32[32,128]{1,0:T(8,128)S(1)} fusion(bf16[128,7200]{0,1:T(8,128)(2,1)S(1)} %copy-done.1, f32[32,7200]{1,0:T(8,128)S(1)} %copy-done.4), kind=kOutput, calls=%fused_computation.6 | convolution fusion | flops 355972096 | bytes 2781184 | tf_op jit(solution)/shard_map/dot_general | solution.py:38
  16.6 0.9 fusion.9
  17.4 6.0 %all-gather.5.cloned.1.call-done = bf16[112,7200]{1,0:T(8,128)(2,1)} async-done(((bf16[56,7200]{1,0:T(8,128)(2,1)}), bf16[112,7200]{1,0:T(8,128)(2,1)}) %all-gather.5.cloned.1.call-update) | async-done | bytes 1612816 | tf_op jit(solution)/shard_map/all_gather | solution.py:49
  23.5 2.3 %fusion.20 = (f32[112]{0:T(128)S(1)}, f32[112,128]{1,0:T(8,128)S(1)}) fusion(f32[112,128]{1,0:T(8,128)} %fusion.9, bf16[112,7200]{1,0:T(8,128)(2,1)} %all-gather.5.cloned.1.call-done, bf16[128,7200]{0,1:T(8,128)(2,1)S(1)} %copy-done.1), kind=kOutput, calls=%fused_computation.40 | convolution fusion | flops 206466960 | bytes 3571136 | tf_op jit(solution)/shard_map/bf,pf->bp/dot_general | solution.py:52
  25.7 0.2 exponential_reduce_fusion
  25.9 0.2 dynamic-update-slice
  26.2 0.2 dynamic-update-slice.1
  26.4 2.4 %all-reduce.3 = (f32[224]{0:T(256)S(1)}, f32[224]{0:T(256)S(1)}) all-reduce(f32[224]{0:T(256)S(1)} %dynamic-update-slice.1, f32[224]{0:T(256)S(1)} %dynamic-update-slice), channel_id=3, replica_groups=mesh['cls'=2,'img'=16] {'cls'}, use_global_device_ids=true, to_apply=%add.1 | all-reduce | flops 448 | bytes 3584
  28.8 0.1 log_add_fusion
  28.9 2.6 %fusion.7 = f32[128,7200]{1,0:T(8,128)} fusion(bf16[112,7200]{1,0:T(8,128)(2,1)S(1)} %copy-done, f32[112,128]{1,0:T(8,128)S(1)} %get-tuple-element.20, f32[112]{0:T(128)S(1)} %log_add_fusion), kind=kOutput, calls=%fused_computation.10 | convolution fusion | flops 206467072 | bytes 5356992 | tf_op jit(solution)/shard_map/bp,bf->pf/dot_general | solution.py:62
  31.5 0.0 all-reduce.6.cloned.1.call-update
  31.6 0.6 copy-done.6
  32.2 0.6 dynamic-slice.2
  33.4 0.6 dynamic_slice.8
  34.0 158.3 %all-reduce.6.cloned.1.call-done = f32[128,7200]{1,0:T(8,128)} async-done(((f32[128,7200]{1,0:T(8,128)}), f32[128,7200]{1,0:T(8,128)}) %all-reduce.6.cloned.1.call-update) | async-done | bytes 3686416
  192.3 1.6 constant_dynamic-slice_fusion
  (23 shorter events, 0.1 us)
Async XLA Ops:
  7.2 5.7 %copy-start.7 = (u32[32]{0:T(128)S(1)}, u32[32]{0:T(128)}, u32[]{:S(2)}) copy-start(u32[32]{0:T(128)} %constant.63) | copy-start | bytes 388
  7.2 3.6 %copy-start.2 = (s32[56]{0:T(128)S(1)}, s32[56]{0:T(128)}, u32[]{:S(2)}) copy-start(s32[56]{0:T(128)} %param.10) | copy-start | bytes 676
  7.2 7.1 %copy-start.4 = (f32[32,7200]{1,0:T(8,128)S(1)}, f32[32,7200]{1,0:T(8,128)}, u32[]{:S(2)}) copy-start(f32[32,7200]{1,0:T(8,128)} %param.8) | copy-start | bytes 2764804
  7.2 3.6 %copy-start.5 = (s32[56]{0:T(128)S(1)}, s32[56]{0:T(128)}, u32[]{:S(2)}) copy-start(s32[56]{0:T(128)} %param.11) | copy-start | bytes 676
  7.2 7.0 %copy-start.3 = (f32[4]{0:T(128)S(1)}, f32[4]{0:T(128)}, u32[]{:S(2)}) copy-start(f32[4]{0:T(128)} %param.9) | copy-start | bytes 52
  7.2 7.1 %copy-start.1 = (bf16[128,7200]{0,1:T(8,128)(2,1)S(1)}, bf16[128,7200]{0,1:T(8,128)(2,1)}, u32[]{:S(2)}) copy-start(bf16[128,7200]{0,1:T(8,128)(2,1)} %param.7) | copy-start | bytes 5529604
  7.2 16.2 %all-gather.5.cloned.1.call-start = ((), (), s32[]{:S(2)}) async-start(), calls=%async_computation | async-start | bytes 2451456 | tf_op jit(solution)/shard_map/all_gather | solution.py:49
  10.7 181.6 %all-reduce.6.cloned.1.call-start = ((), (), s32[]{:S(2)}) async-start(), calls=%async_computation.1 | async-start | bytes 7471104
  23.5 5.5 %copy-start = (bf16[112,7200]{1,0:T(8,128)(2,1)S(1)}, bf16[112,7200]{1,0:T(8,128)(2,1)}, u32[]{:S(2)}) copy-start(bf16[112,7200]{1,0:T(8,128)(2,1)} %all-gather.5.cloned.1.call-done) | copy-start | bytes 4838404
  31.5 0.7 copy-start.6
Sparse Core Ops, SparseCore 0:
  10.8 12.6 all-gather.4
  31.7 160.5 all-reduce.5
where the time goes:
time: 201 us
  waiting for transfers between devices  164 us (82%)
  between operations  15.5 us (8%)
  matrix products  11.4 us (6%)
  local copies, waits for them, and re-layouts  4.61 us (2%)
  blocking collectives  4.41 us (2%)
    unnamed x3, waiting for transfers between devices  158 us
    all_gather x1, waiting for transfers between devices, body(): lax.all_gather(whitened, 'cls', axis=0, tiled=True)  6.04 us
  transfers between devices with their start and end apart: 2, of which 2 were waited for; matrix products, arithmetic and copies ran while one was open for 3% of the time, Pallas kernels for 0%

commit v1 on v0

v1 whole, which is shorter than its diff:
```python
import jax
import jax.numpy as jnp
from jax import lax
from jax.sharding import PartitionSpec as P

LANES = 128


def group_of(members):
    return next(size for size in (4, 2, 1) if members % size == 0)


def shifted(value, axis, step):
    count = lax.axis_size(axis)
    return lax.ppermute(value, axis, [(place, (place + step) % count) for place in range(count)])


def crossed(value, axis, flip):
    count = lax.axis_size(axis)
    return lax.ppermute(value, axis, [(place, place ^ flip) for place in range(count)])


def gathered_from(value, axis):
    return [value] + [shifted(value, axis, step) for step in range(1, lax.axis_size(axis))]


def body(images, projections, noise_power, class_logprior, groups, offsets):
    rows_here, terms = images.shape
    proj_here = projections.shape[0]
    cycle_size = lax.axis_size("cls")
    cycle_place = lax.axis_index("cls")
    owners = lax.axis_size("img")
    team = group_of(owners)
    member = lax.axis_index("img") % team
    width = -(-terms // (LANES * team)) * LANES
    group_count = noise_power.shape[0]
    class_count = class_logprior.shape[0]
    inverse = 1.0 / noise_power
    group_hot = (groups[:, None] == jnp.arange(group_count, dtype=jnp.int32)[None, :]).astype(
        jnp.float32
    )
    offset_hot = (offsets[:, None] == jnp.arange(class_count, dtype=jnp.int32)[None, :]).astype(
        jnp.float32
    )
    row_inverse = jnp.dot(group_hot, inverse, precision=lax.Precision.HIGHEST)
    whitened = (images.astype(jnp.float32) * row_inverse).astype(jnp.bfloat16)
    tag_rows = jnp.concatenate([group_hot, offset_hot], axis=1).astype(jnp.bfloat16)

    gathered = jnp.concatenate(gathered_from(whitened, "cls"), axis=0)
    labels = jnp.concatenate(gathered_from(tag_rows, "cls"), axis=0)
    padded = jnp.pad(whitened, ((0, 0), (0, width * team - terms)))
    parts = [
        lax.dynamic_slice_in_dim(padded, (member ^ flip) * width, width, axis=1)
        for flip in range(team)
    ]
    slab_own = jnp.concatenate(
        [parts[0]] + [crossed(parts[flip], "img", flip) for flip in range(1, team)], axis=0
    )
    slabs = gathered_from(slab_own, "cls")

    proj_float = projections.astype(jnp.float32)
    quadratic = jnp.dot(inverse, (proj_float * proj_float).T, precision=lax.Precision.HIGHEST)
    global_index = cycle_place * proj_here + jnp.arange(proj_here, dtype=jnp.int32)
    per_class = proj_here * cycle_size // class_count
    class_of = global_index // per_class
    class_shift = (
        class_of[None, :] - jnp.arange(class_count, dtype=jnp.int32)[:, None]
    ) % class_count
    matches = class_shift[:, :, None] == jnp.arange(class_count, dtype=jnp.int32)[None, None, :]
    prior_table = jnp.sum(jnp.where(matches, class_logprior[None, None, :], 0.0), axis=2)
    bias_table = jnp.concatenate([-0.5 * quadratic, prior_table], axis=0)
    products = jnp.einsum("bf,pf->bp", gathered, projections, preferred_element_type=jnp.float32)
    scores = products + jnp.dot(
        labels.astype(jnp.float32), bias_table, precision=lax.Precision.HIGHEST
    )
    local_peak = jnp.max(scores, axis=1)
    local_sum = jnp.sum(jnp.exp(scores - local_peak[:, None]), axis=1)
    stats = jnp.stack([local_peak, local_sum]).reshape(2, cycle_size, rows_here)
    peak, exp_sum = stats[0], stats[1]
    for step in range(1, cycle_size):
        turned = jnp.roll(stats, step, axis=1)
        other = shifted(turned, "cls", step)
        top = jnp.maximum(peak, other[0])
        exp_sum = exp_sum * jnp.exp(peak - top) + other[1] * jnp.exp(other[0] - top)
        peak = top
    evidence = (peak + jnp.log(exp_sum)).reshape(cycle_size * rows_here)
    posterior = jnp.exp(scores - evidence[:, None]).astype(jnp.bfloat16)
    weights = posterior[None]
    flip = 1
    while flip < team:
        weights = jnp.concatenate([weights, crossed(weights, "img", flip)], axis=0)
        flip *= 2
    weights = weights.reshape(team, cycle_size, rows_here, proj_here)
    sums = sum(
        jnp.einsum(
            "bp,bf->pf",
            weights[:, place].reshape(team * rows_here, proj_here),
            slabs[place],
            preferred_element_type=jnp.float32,
        )
        for place in range(cycle_size)
    )
    blocks = sums.astype(jnp.bfloat16).reshape(owners, proj_here // owners, width)
    pieces = lax.all_to_all(blocks, "img", 0, 0)
    pieces = pieces.reshape(owners // team, team, proj_here // owners, width)
    total = jnp.sum(pieces.astype(jnp.float32), axis=0)
    sum_rows = jnp.concatenate([total[place] for place in range(team)], axis=1)[:, :terms]
    return (sum_rows, evidence[:rows_here])


def solution(mesh):
    in_specs = (
        P(("cls", "img"), None),
        P("cls", None),
        P(),
        P(),
        P(("cls", "img")),
        P(("cls", "img")),
    )
    out_specs = (P(("cls", "img"), None), P(("cls", "img")))
    return jax.shard_map(body, mesh=mesh, in_specs=in_specs, out_specs=out_specs, check_vma=False)
```

time: 201 us -> 49.8 us (0.25)
  waiting for transfers between devices: 164 us -> 21.6 us
  between operations: 15.5 us -> 0.86 us
  starting transfers between devices: 0.08 us -> 14.1 us
  blocking collectives: 4.41 us -> 0 us
  local copies, waits for them, and re-layouts: 4.61 us -> 1.28 us
  matrix products: 11.4 us -> 9.02 us
  other arithmetic: 0.41 us -> 2.72 us
    unnamed x3 -> x0, waiting for transfers between devices: 158 us -> none
    all_to_all x0 -> x1, waiting for transfers between devices: none -> 12.2 us  [body(): pieces = lax.all_to_all(blocks, 'img', 0, 0)]
    ppermute x0 -> x9, waiting for transfers between devices: none -> 9.37 us  [the longest x5 9.36 us: crossed(): lax.ppermute(value, axis, [(place, place ^ flip) for place in range(count)])]
    ppermute x0 -> x9, starting transfers between devices: none -> 8.19 us  [the longest x5 7.41 us: crossed(): lax.ppermute(value, axis, [(place, place ^ flip) for place in range(count)])]
    all_gather x1 -> x0, waiting for transfers between devices: 6.04 us -> none  [body(): lax.all_gather(whitened, 'cls', axis=0, tiled=True)]
    all_to_all x0 -> x1, starting transfers between devices: none -> 5.92 us  [body(): pieces = lax.all_to_all(blocks, 'img', 0, 0)]
    unnamed x24 -> x5, local copies, waits for them, and re-layouts: 4.01 us -> 0.01 us
    unnamed x1 -> x0, blocking collectives: 2.44 us -> none
  transfers between devices with their start and end apart: 2 -> 10, of which waited for: 2 -> 4; matrix products, arithmetic and copies ran while one was open for 3% -> 19% of each run, Pallas kernels for 0% -> 0%
where the time goes in v1:
time: 49.8 us; the launch traced here: 49.6 us
  waiting for transfers between devices  21.6 us (43%)
  starting transfers between devices  14.1 us (28%)
  matrix products  9.02 us (18%)
  other arithmetic  2.72 us (5%)
  local copies, waits for them, and re-layouts  1.28 us (3%)
  between operations  0.86 us (2%)
    all_to_all x1, waiting for transfers between devices, body(): pieces = lax.all_to_all(blocks, 'img', 0, 0)  12.2 us
    ppermute x5, waiting for transfers between devices, crossed(): lax.ppermute(value, axis, [(place, place ^ flip) for place in range(count)])  9.36 us
    ppermute x5, starting transfers between devices, crossed(): lax.ppermute(value, axis, [(place, place ^ flip) for place in range(count)])  7.41 us
    all_to_all x1, starting transfers between devices, body(): pieces = lax.all_to_all(blocks, 'img', 0, 0)  5.92 us
    dot_general x1, matrix products, body(): jnp.dot(inverse, (proj_float * proj_float).T, precision=lax.Precision.HIG...  4.2 us
    dot_general x1, matrix products, body(): row_inverse = jnp.dot(group_hot, inverse, precision=lax.Precision.HIGHEST)  2.35 us
    dot_general x2, matrix products, body(): jnp.einsum('bp,bf->pf', weights[:, place].reshape(team * rows_here, proj_...  1.45 us
  transfers between devices with their start and end apart: 10, of which 4 were waited for; matrix products, arithmetic and copies ran while one was open for 19% of the time, Pallas kernels for 0%

profile of v1, /device:TPU:0, one launch (start us, length us, event | category | flops | bytes accessed | tf_op | source)
XLA Modules:
  0.0 49.6 jit_solution(4391297329058170083)
XLA Ops:
  0.6 0.7 %iota_compare_fusion.2 = pred[56,4]{0,1:T(4,128)(4,1)S(1)} fusion(s32[56]{0:T(128)} %param.11), kind=kLoop, calls=%fused_computation.50 | loop fusion | flops 224 | bytes 448 | tf_op jit(solution)/shard_map/eq | solution.py:42
  1.3 0.7 %iota_compare_fusion = pred[56,32]{0,1:T(8,128)(4,1)S(1)} fusion(s32[56]{0:T(128)} %param.10), kind=kLoop, calls=%fused_computation.37 | loop fusion | flops 1792 | bytes 2016 | tf_op jit(solution)/shard_map/eq | solution.py:39
  2.0 0.6 %collective-permute-start.1 = (bf16[56,36]{0,1:T(8,128)(2,1)S(1)}, bf16[56,36]{0,1:T(8,128)(2,1)S(1)}, u32[]{:S(2)}, u32[]{:S(2)}) collective-permute-start(bf16[56,36]{0,1:T(8,128)(2,1)S(1)} %convert_convert_fusion), channel_id=1, source_target_pairs={{0,16},{16,0},{1,17},{17,1},{2,18},{18,2},{3,19},{19,3},{4,20},{20... | collective-permute-start | bytes 12104 | tf_op jit(solution)/shard_map/ppermute | solution.py:15
  2.5 2.3 %fusion = bf16[56,7200]{1,0:T(8,128)(2,1)S(1)} fusion(bf16[56,7200]{1,0:T(8,128)(2,1)} %param.6, f32[32,7200]{1,0:T(8,128)} %param.8, s32[56]{0:T(128)} %param.10), kind=kOutput, calls=%fused_computation.1 | convolution fusion | flops 156270592 | bytes 2534624 | tf_op jit(solution)/shard_map/dot_general | solution.py:45
  5.0 0.2 pad_dynamic-slice_fusion.3
  5.2 3.0 %collective-permute-start.5 = (bf16[56,1920]{1,0:T(8,128)(2,1)S(1)}, bf16[56,1920]{1,0:T(8,128)(2,1)S(1)}, u32[]{:S(2)}, u32[]{:S(2)}) collective-permute-start(bf16[56,1920]{1,0:T(8,128)(2,1)S(1)} %get-tuple-element.3), channel_id=1, source_target_pairs={{0,1},{1,0},{2,3},{3,2},{4,5},{5,4},{6,7},{7,6},{8,9},{9,8},{10,11... | collective-permute-start | bytes 645128 | tf_op jit(solution)/shard_map/ppermute | solution.py:20
  8.2 1.5 %collective-permute-start.6 = (bf16[56,1920]{1,0:T(8,128)(2,1)S(1)}, bf16[56,1920]{1,0:T(8,128)(2,1)S(1)}, u32[]{:S(2)}, u32[]{:S(2)}) collective-permute-start(bf16[56,1920]{1,0:T(8,128)(2,1)S(1)} %get-tuple-element.4), channel_id=1, source_target_pairs={{0,2},{1,3},{2,0},{3,1},{4,6},{5,7},{6,4},{7,5},{8,10},{9,11},{10,... | collective-permute-start | bytes 645128 | tf_op jit(solution)/shard_map/ppermute | solution.py:20
  9.8 4.2 %fusion.13 = f32[32,128]{1,0:T(8,128)S(1)} fusion(bf16[128,7200]{0,1:T(8,128)(2,1)} %param.7, f32[32,7200]{1,0:T(8,128)} %param.8), kind=kOutput, calls=%fused_computation.13 | convolution fusion | flops 355972096 | bytes 2781184 | tf_op jit(solution)/shard_map/dot_general | solution.py:62
  14.1 0.3 fusion.16
  14.4 0.7 %fusion.41 = (f32[112]{0:T(128)S(1)}, f32[112,128]{1,0:T(8,128)S(1)}) fusion(f32[112,128]{1,0:T(8,128)S(1)} %fusion.16, bf16[128,7200]{0,1:T(8,128)(2,1)S(1)} %copy-done.1, bf16[56,7200]{1,0:T(8,128)(2,1)S(1)} %collective-permute-done, bf16[56,7200]{1,0:T(8,128)(2,1)S(1)} %fusion), kind=kOutput, calls=%fused_computation.78 | convolution fusion | flops 209692560 | bytes 3571136 | tf_op jit(solution)/shard_map/bf,pf->bp/dot_general | solution.py:72
  15.2 0.2 exponential_reduce_fusion
  15.6 4.2 %collective-permute-done.6 = bf16[56,1920]{1,0:T(8,128)(2,1)S(1)} collective-permute-done((bf16[56,1920]{1,0:T(8,128)(2,1)S(1)}, bf16[56,1920]{1,0:T(8,128)(2,1)S(1)}, u32[]{:S(2)}, u32[]{:S(2)}) %collective-permute-start.6) | collective-permute-done | bytes 215072 | tf_op jit(solution)/shard_map/ppermute | solution.py:20
  20.1 0.1 fusion.47
  20.2 1.3 %collective-permute-start.3 = (bf16[1,112,128]{2,1,0:T(8,128)(2,1)S(1)}, bf16[1,112,128]{2,1,0:T(8,128)(2,1)S(1)}, u32[]{:S(2)}, u32[]{:S(2)}) collective-permute-start(bf16[1,112,128]{2,1,0:T(8,128)(2,1)S(1)} %fusion.47), channel_id=1, source_target_pairs={{0,1},{1,0},{2,3},{3,2},{4,5},{5,4},{6,7},{7,6},{8,9},{9,8},{10,11... | collective-permute-start | bytes 86024 | tf_op jit(solution)/shard_map/ppermute | solution.py:20
  21.5 2.6 %collective-permute-done.3 = bf16[1,112,128]{2,1,0:T(8,128)(2,1)S(1)} collective-permute-done((bf16[1,112,128]{2,1,0:T(8,128)(2,1)S(1)}, bf16[1,112,128]{2,1,0:T(8,128)(2,1)S(1)}, u32[]{:S(2)}, u32[]{:S(2)}) %collective-permute-start.3) | collective-permute-done | bytes 28704 | tf_op jit(solution)/shard_map/ppermute | solution.py:20
  24.2 1.6 %collective-permute-start.4 = (bf16[2,112,128]{2,1,0:T(8,128)(2,1)S(1)}, bf16[2,112,128]{2,1,0:T(8,128)(2,1)S(1)}, u32[]{:S(2)}, u32[]{:S(2)}) collective-permute-start(bf16[2,112,128]{2,1,0:T(8,128)(2,1)S(1)} %pad_maximum_fusion.5), channel_id=1, source_target_pairs={{0,2},{1,3},{2,0},{3,1},{4,6},{5,7},{6,4},{7,5},{8,10},{9,11},{10,... | collective-permute-start | bytes 172040 | tf_op jit(solution)/shard_map/ppermute | solution.py:20
  25.8 0.1 exponential_convert_fusion
  25.9 2.6 %collective-permute-done.4 = bf16[2,112,128]{2,1,0:T(8,128)(2,1)S(1)} collective-permute-done((bf16[2,112,128]{2,1,0:T(8,128)(2,1)S(1)}, bf16[2,112,128]{2,1,0:T(8,128)(2,1)S(1)}, u32[]{:S(2)}, u32[]{:S(2)}) %collective-permute-start.4) | collective-permute-done | bytes 57376 | tf_op jit(solution)/shard_map/ppermute | solution.py:20
  28.5 0.3 fusion.42
  28.8 1.1 %fusion.5 = bf16[16,8,1920]{2,1,0:T(8,128)(2,1)} fusion(f32[128,1920]{1,0:T(8,128)S(1)} %fusion.42, bf16[224,128]{1,0:T(8,128)(2,1)S(1)} %bitcast.54, bf16[56,1920]{1,0:T(8,128)(2,1)S(1)} %collective-permute-done.7, bf16[56,1920]{1,0:T(8,128)(2,1)S(1)} %collective-permute-done.6, bf16[56,1920]{1,0:T(8,128)(2,1)S(1)} %collective-permute-done.5, ...), kind=kOutput, calls=%fused_computation.7 | convolution fusion | flops 114032640 | bytes 2392064 | tf_op jit(solution)/shard_map/bp,bf->pf/dot_general | solution.py:95
  29.9 5.9 %all-to-all-start = ((bf16[16,8,1920]{2,1,0:T(8,128)(2,1)}), bf16[16,8,1920]{2,1,0:T(8,128)(2,1)S(1)}, u32[]{:S(2)}, u32[]{:S(2)}) async-start(bf16[16,8,1920]{2,1,0:T(8,128)(2,1)} %fusion.5), calls=%async_computation | async-start | bytes 983040 | tf_op jit(solution)/shard_map/all_to_all | solution.py:104
  36.0 0.5 %slice_bitcast_fusion.4 = f32[56]{0:T(128)} fusion(f32[2,56]{1,0:T(2,128)S(1)} %fusion.26), kind=kLoop, calls=%fused_computation.65 | loop fusion | bytes 448 | tf_op jit(solution)/shard_map/slice | solution.py:108
  36.6 12.2 %all-to-all-done = bf16[16,8,1920]{2,1,0:T(8,128)(2,1)S(1)} async-done(((bf16[16,8,1920]{2,1,0:T(8,128)(2,1)}), bf16[16,8,1920]{2,1,0:T(8,128)(2,1)S(1)}, u32[]{:S(2)}, u32[]{:S(2)}) %all-to-all-start) | async-done | bytes 491552 | tf_op jit(solution)/shard_map/all_to_all | solution.py:104
  48.9 0.7 %pad_maximum_fusion.1 = f32[8,7200]{1,0:T(8,128)} fusion(f32[8,1920]{1,0:T(8,128)S(1)} %get-tuple-element.7, f32[8,1920]{1,0:T(8,128)S(1)} %get-tuple-element.8, f32[8,1920]{1,0:T(8,128)S(1)} %get-tuple-element.9, f32[8,1920]{1,0:T(8,128)S(1)} %get-tuple-element.6), kind=kLoop, calls=%fused_computation.21 | loop fusion | flops 172800 | bytes 476160 | tf_op jit(solution)/shard_map/concatenate | solution.py:107
  (37 shorter events, 1.1 us)
Async XLA Ops:
  2.0 12.1 %collective-permute-start.1 = (bf16[56,36]{0,1:T(8,128)(2,1)S(1)}, bf16[56,36]{0,1:T(8,128)(2,1)S(1)}, u32[]{:S(2)}, u32[]{:S(2)}) collective-permute-start(bf16[56,36]{0,1:T(8,128)(2,1)S(1)} %convert_convert_fusion), channel_id=1, source_target_pairs={{0,16},{16,0},{1,17},{17,1},{2,18},{18,2},{3,19},{19,3},{4,20},{20... | collective-permute-start | bytes 12104 | tf_op jit(solution)/shard_map/ppermute | solution.py:15
  4.9 9.5 %collective-permute-start = (bf16[56,7200]{1,0:T(8,128)(2,1)S(1)}, bf16[56,7200]{1,0:T(8,128)(2,1)S(1)}, u32[]{:S(2)}, u32[]{:S(2)}) collective-permute-start(bf16[56,7200]{1,0:T(8,128)(2,1)S(1)} %fusion), channel_id=1, source_target_pairs={{0,16},{16,0},{1,17},{17,1},{2,18},{18,2},{3,19},{19,3},{4,20},{20... | collective-permute-start | bytes 2419208 | tf_op jit(solution)/shard_map/ppermute | solution.py:15
  5.2 10.4 %collective-permute-start.5 = (bf16[56,1920]{1,0:T(8,128)(2,1)S(1)}, bf16[56,1920]{1,0:T(8,128)(2,1)S(1)}, u32[]{:S(2)}, u32[]{:S(2)}) collective-permute-start(bf16[56,1920]{1,0:T(8,128)(2,1)S(1)} %get-tuple-element.3), channel_id=1, source_target_pairs={{0,1},{1,0},{2,3},{3,2},{4,5},{5,4},{6,7},{7,6},{8,9},{9,8},{10,11... | collective-permute-start | bytes 645128 | tf_op jit(solution)/shard_map/ppermute | solution.py:20
  8.2 11.6 %collective-permute-start.6 = (bf16[56,1920]{1,0:T(8,128)(2,1)S(1)}, bf16[56,1920]{1,0:T(8,128)(2,1)S(1)}, u32[]{:S(2)}, u32[]{:S(2)}) collective-permute-start(bf16[56,1920]{1,0:T(8,128)(2,1)S(1)} %get-tuple-element.4), channel_id=1, source_target_pairs={{0,2},{1,3},{2,0},{3,1},{4,6},{5,7},{6,4},{7,5},{8,10},{9,11},{10,... | collective-permute-start | bytes 645128 | tf_op jit(solution)/shard_map/ppermute | solution.py:20
  9.7 10.1 %collective-permute-start.7 = (bf16[56,1920]{1,0:T(8,128)(2,1)S(1)}, bf16[56,1920]{1,0:T(8,128)(2,1)S(1)}, u32[]{:S(2)}, u32[]{:S(2)}) collective-permute-start(bf16[56,1920]{1,0:T(8,128)(2,1)S(1)} %get-tuple-element.5), channel_id=1, source_target_pairs={{0,3},{1,2},{2,1},{3,0},{4,7},{5,6},{6,5},{7,4},{8,11},{9,10},{10,... | collective-permute-start | bytes 645128 | tf_op jit(solution)/shard_map/ppermute | solution.py:20
  9.8 4.2 %copy-start = (f32[4]{0:T(128)S(1)}, f32[4]{0:T(128)}, u32[]{:S(2)}) copy-start(f32[4]{0:T(128)} %param.9) | copy-start | bytes 52
  9.8 4.6 %copy-start.1 = (bf16[128,7200]{0,1:T(8,128)(2,1)S(1)}, bf16[128,7200]{0,1:T(8,128)(2,1)}, u32[]{:S(2)}) copy-start(bf16[128,7200]{0,1:T(8,128)(2,1)} %param.7) | copy-start | bytes 5529604
  15.5 4.4 %collective-permute-start.2 = (f32[2,2,56]{2,1,0:T(2,128)S(1)}, f32[2,2,56]{2,1,0:T(2,128)S(1)}, u32[]{:S(2)}, u32[]{:S(2)}) collective-permute-start(f32[2,2,56]{2,1,0:T(2,128)S(1)} %pad_maximum_fusion.6), channel_id=1, source_target_pairs={{0,16},{16,0},{1,17},{17,1},{2,18},{18,2},{3,19},{19,3},{4,20},{20... | collective-permute-start | bytes 2696 | tf_op jit(solution)/shard_map/ppermute | solution.py:15
  19.9 8.6 %collective-permute-start.8 = (bf16[224,1920]{1,0:T(8,128)(2,1)S(1)}, bf16[224,1920]{1,0:T(8,128)(2,1)S(1)}, u32[]{:S(2)}, u32[]{:S(2)}) collective-permute-start(bf16[224,1920]{1,0:T(8,128)(2,1)S(1)} %pad_maximum_fusion), channel_id=1, source_target_pairs={{0,16},{16,0},{1,17},{17,1},{2,18},{18,2},{3,19},{19,3},{4,20},{20... | collective-permute-start | bytes 2580488 | tf_op jit(solution)/shard_map/ppermute | solution.py:15
  20.2 3.9 %collective-permute-start.3 = (bf16[1,112,128]{2,1,0:T(8,128)(2,1)S(1)}, bf16[1,112,128]{2,1,0:T(8,128)(2,1)S(1)}, u32[]{:S(2)}, u32[]{:S(2)}) collective-permute-start(bf16[1,112,128]{2,1,0:T(8,128)(2,1)S(1)} %fusion.47), channel_id=1, source_target_pairs={{0,1},{1,0},{2,3},{3,2},{4,5},{5,4},{6,7},{7,6},{8,9},{9,8},{10,11... | collective-permute-start | bytes 86024 | tf_op jit(solution)/shard_map/ppermute | solution.py:20
  24.2 4.2 %collective-permute-start.4 = (bf16[2,112,128]{2,1,0:T(8,128)(2,1)S(1)}, bf16[2,112,128]{2,1,0:T(8,128)(2,1)S(1)}, u32[]{:S(2)}, u32[]{:S(2)}) collective-permute-start(bf16[2,112,128]{2,1,0:T(8,128)(2,1)S(1)} %pad_maximum_fusion.5), channel_id=1, source_target_pairs={{0,2},{1,3},{2,0},{3,1},{4,6},{5,7},{6,4},{7,5},{8,10},{9,11},{10,... | collective-permute-start | bytes 172040 | tf_op jit(solution)/shard_map/ppermute | solution.py:20
  29.9 18.8 %all-to-all-start = ((bf16[16,8,1920]{2,1,0:T(8,128)(2,1)}), bf16[16,8,1920]{2,1,0:T(8,128)(2,1)S(1)}, u32[]{:S(2)}, u32[]{:S(2)}) async-start(bf16[16,8,1920]{2,1,0:T(8,128)(2,1)} %fusion.5), calls=%async_computation | async-start | bytes 983040 | tf_op jit(solution)/shard_map/all_to_all | solution.py:104

commit v2 on v1

v2 whole, which is shorter than its diff:
```python
import functools

import jax
import jax.numpy as jnp
from jax import lax
from jax.experimental import pallas as pl
from jax.experimental.pallas import tpu as pltpu
from jax.sharding import PartitionSpec as P

LANES = 128
PARTS = 3
GRANT = 24 * 2**20


def group_of(members):
    return next(size for size in (4, 2, 1) if members % size == 0)


def shifted(value, axis, step):
    count = lax.axis_size(axis)
    return lax.ppermute(value, axis, [(place, (place + step) % count) for place in range(count)])


def crossed(value, axis, flip):
    count = lax.axis_size(axis)
    return lax.ppermute(value, axis, [(place, place ^ flip) for place in range(count)])


def gathered_from(value, axis):
    return [value] + [shifted(value, axis, step) for step in range(1, lax.axis_size(axis))]


def split(value, count):
    pieces = []
    for _ in range(count):
        piece = value.astype(jnp.bfloat16)
        pieces.append(piece)
        value = value - piece.astype(jnp.float32)
    return pieces


def first_rows(left, right):
    return lax.dot_general(left, right, (((0,), (0,)), ((), ())), preferred_element_type=jnp.float32)


def column_of(shape, start):
    return start + lax.broadcasted_iota(jnp.int32, shape, 1)


def whiten_kernel(terms, tag_column, groups_ref, offsets_ref, images_ref, noise_ref, out_ref, *, classes):
    step = pl.program_id(0)
    rows, width = out_ref.shape
    group_count = noise_ref.shape[0]

    def hot(ids, count):
        places = lax.broadcasted_iota(jnp.int32, (count, rows), 0)
        return jnp.where(places == ids, 1.0, 0.0)

    group_hot = hot(groups_ref[...], group_count).astype(jnp.bfloat16)
    pieces = split(1.0 / noise_ref[...], PARTS)
    row_inverse = first_rows(
        jnp.concatenate([group_hot] * PARTS, axis=0), jnp.concatenate(pieces, axis=0)
    )
    white = images_ref[...].astype(jnp.float32) * row_inverse
    last = pl.num_programs(0) - 1

    @pl.when(step != last)
    def _():
        out_ref[...] = white.astype(jnp.bfloat16)

    @pl.when(step == last)
    def _():
        start = last * width
        kept = jnp.where(column_of((rows, width), start) < terms, white, 0.0)
        out_ref[...] = kept.astype(jnp.bfloat16)
        tile = tag_column // LANES * LANES
        for ids, count, shift in (
            (groups_ref[...], group_count, tag_column - tile),
            (offsets_ref[...], classes, tag_column - tile + group_count),
        ):
            tall = -(-count // 16) * 16
            line = lax.broadcasted_iota(jnp.int32, (tall, LANES), 0)
            lane = lax.broadcasted_iota(jnp.int32, (tall, LANES), 1)
            spread = jnp.where(lane == line + shift, 1.0, 0.0).astype(jnp.bfloat16)
            mark = first_rows(hot(ids, tall).astype(jnp.bfloat16), spread)
            place = pl.ds(tile - start, LANES)
            out_ref[:, place] = out_ref[:, place] + mark.astype(jnp.bfloat16)


def table_kernel(shift, per_class, place_ref, prior_ref, noise_ref, tall_ref, out_ref):
    group_count = noise_ref.shape[0]
    proj_here = tall_ref.shape[1]
    class_count = prior_ref.shape[0]
    tall = tall_ref[...].astype(jnp.float32)
    high, low = split(tall * tall, 2)
    narrow = jnp.concatenate(split(1.0 / noise_ref[...], 2), axis=0)
    both = jnp.dot(narrow, high, preferred_element_type=jnp.float32) + jnp.dot(
        narrow, low, preferred_element_type=jnp.float32
    )
    out_ref[...] = jnp.zeros_like(out_ref)
    out_ref[pl.ds(shift, group_count), :] = -0.5 * (both[:group_count] + both[group_count:])
    index = place_ref[0] * proj_here + lax.broadcasted_iota(jnp.int32, (1, proj_here), 1)
    class_of = jnp.zeros_like(index)
    for bound in range(1, class_count):
        class_of = class_of + jnp.where(index >= bound * per_class, 1, 0)
    for offset in range(class_count):
        away = class_of - offset
        away = jnp.where(away < 0, away + class_count, away)
        row = jnp.zeros((1, proj_here), jnp.float32)
        for distance in range(class_count):
            row = jnp.where(away == distance, prior_ref[distance], row)
        out_ref[pl.ds(shift + group_count + offset, 1), :] = row


def score_kernel(tag_column, count, *refs):
    white_refs = refs[:count]
    tall_ref, table_ref, scores_ref, stats_ref = refs[count:]
    terms, proj_here = tall_ref.shape
    tile = tag_column // LANES * LANES
    rows = jnp.concatenate([ref[:, :tile] for ref in white_refs], axis=0)
    marks = jnp.concatenate([ref[:, tile : tile + LANES] for ref in white_refs], axis=0)
    high, *rest = split(table_ref[...], PARTS)
    if tile < terms:
        high = jnp.concatenate([tall_ref[tile:, :], high[terms - tile :]], axis=0)
    scores = jnp.dot(rows, tall_ref[:tile, :], preferred_element_type=jnp.float32)
    bias = sum(jnp.dot(marks, piece, preferred_element_type=jnp.float32) for piece in rest)
    scores = scores + (jnp.dot(marks, high, preferred_element_type=jnp.float32) + bias)
    peak = jnp.max(scores, axis=1, keepdims=True)
    weight = jnp.sum(jnp.exp(scores - peak), axis=1, keepdims=True)
    scores_ref[...] = scores
    lane = lax.broadcasted_iota(jnp.int32, stats_ref.shape, 1)
    stats_ref[...] = jnp.where(lane == 0, peak, weight)


def posterior_kernel(count, rows_here, *refs):
    scores_ref = refs[0]
    stats_refs = refs[1 : 1 + count]
    posterior_ref, evidence_ref = refs[1 + count :]
    for place in range(count):
        mine = pl.ds(place * rows_here, rows_here)
        peak = stats_refs[0][mine, 0:1]
        weight = stats_refs[0][mine, 1:2]
        for step in range(1, count):
            theirs = pl.ds((place - step) % count * rows_here, rows_here)
            other_peak = stats_refs[step][theirs, 0:1]
            other_weight = stats_refs[step][theirs, 1:2]
            top = jnp.maximum(peak, other_peak)
            weight = weight * jnp.exp(peak - top) + other_weight * jnp.exp(other_peak - top)
            peak = top
        evidence = peak + jnp.log(weight)
        posterior_ref[mine, :] = jnp.exp(scores_ref[mine, :] - evidence).astype(jnp.bfloat16)
        if place == 0:
            evidence_ref[...] = jnp.broadcast_to(evidence, evidence_ref.shape)


def sums_kernel(team, count, *refs):
    weight_refs, slab_refs, out_ref = refs[:team], refs[team:-1], refs[-1]
    rows_here = weight_refs[0].shape[0] // count
    weights = [
        ref[pl.ds(place * rows_here, rows_here), :]
        for place in range(count)
        for ref in weight_refs
    ]
    slabs = [ref[...] for ref in slab_refs]
    out_ref[...] = first_rows(
        jnp.concatenate(weights, axis=0), jnp.concatenate(slabs, axis=0)
    ).astype(out_ref.dtype)


def body(images, projections, noise_power, class_logprior, groups, offsets):
    rows_here, terms = images.shape
    proj_here = projections.shape[0]
    cycle_size = lax.axis_size("cls")
    cycle_place = lax.axis_index("cls")
    owners = lax.axis_size("img")
    team = group_of(owners)
    member = lax.axis_index("img") % team
    group_count = noise_power.shape[0]
    class_count = class_logprior.shape[0]
    tags = group_count + class_count
    tag_column = terms if terms % LANES + tags <= LANES else -(-terms // LANES) * LANES
    width = -(-(tag_column + tags) // (LANES * team)) * LANES
    per_class = proj_here * cycle_size // class_count
    all_rows = cycle_size * rows_here
    columns = functools.partial(pl.BlockSpec, index_map=lambda j: (0, j))
    still = functools.partial(pl.BlockSpec, index_map=lambda j: (0, 0))
    grant = functools.partial(pltpu.CompilerParams, vmem_limit_bytes=GRANT)
    scalars = pl.BlockSpec(memory_space=pltpu.SMEM)
    local = pl.BlockSpec(memory_space=pltpu.VMEM)

    whitened = pl.pallas_call(
        functools.partial(whiten_kernel, terms, tag_column, classes=class_count),
        out_shape=jax.ShapeDtypeStruct((rows_here, team * width), jnp.bfloat16),
        grid=(team,),
        in_specs=[
            still((1, rows_here)),
            still((1, rows_here)),
            columns((rows_here, width)),
            columns((group_count, width)),
        ],
        out_specs=columns((rows_here, width)),
        compiler_params=grant(dimension_semantics=("arbitrary",)),
        cost_estimate=pl.CostEstimate(
            flops=2 * rows_here * PARTS * group_count * terms,
            bytes_accessed=4 * rows_here * terms + 4 * group_count * terms,
            transcendentals=0,
        ),
        name="whiten",
    )(groups.reshape(1, rows_here), offsets.reshape(1, rows_here), images, noise_power)

    tall = projections.T
    table = pl.pallas_call(
        functools.partial(table_kernel, tag_column % LANES, per_class),
        out_shape=jax.ShapeDtypeStruct((LANES, proj_here), jnp.float32),
        in_specs=[scalars, scalars, local, local],
        out_specs=local,
        cost_estimate=pl.CostEstimate(
            flops=8 * proj_here * group_count * terms,
            bytes_accessed=2 * proj_here * terms + 4 * group_count * terms,
            transcendentals=0,
        ),
        compiler_params=grant(),
        name="table",
    )(cycle_place.reshape(1), class_logprior, noise_power, tall)

    gathered = gathered_from(whitened, "cls")
    parts = [
        lax.dynamic_slice_in_dim(whitened, (member ^ flip) * width, width, axis=1)
        for flip in range(team)
    ]
    swapped = [parts[0]] + [crossed(parts[flip], "img", flip) for flip in range(1, team)]

    scores, stats = pl.pallas_call(
        functools.partial(score_kernel, tag_column, cycle_size),
        out_shape=(
            jax.ShapeDtypeStruct((all_rows, proj_here), jnp.float32),
            jax.ShapeDtypeStruct((all_rows, LANES), jnp.float32),
        ),
        in_specs=[local] * (cycle_size + 2),
        out_specs=(local, local),
        cost_estimate=pl.CostEstimate(
            flops=2 * all_rows * proj_here * terms,
            bytes_accessed=2 * (all_rows + proj_here) * terms,
            transcendentals=all_rows * proj_here,
        ),
        compiler_params=grant(),
        name="scores",
    )(*gathered, tall, table)

    posterior, evidence = pl.pallas_call(
        functools.partial(posterior_kernel, cycle_size, rows_here),
        out_shape=(
            jax.ShapeDtypeStruct((all_rows, proj_here), jnp.bfloat16),
            jax.ShapeDtypeStruct((rows_here, LANES), jnp.float32),
        ),
        in_specs=[local] * (cycle_size + 1),
        out_specs=(local, local),
        compiler_params=grant(),
        name="posterior",
    )(scores, *gathered_from(stats, "cls"))

    weights = [posterior] + [crossed(posterior, "img", flip) for flip in range(1, team)]
    swapped, _ = lax.optimization_barrier((swapped, posterior))
    arrived = jnp.concatenate(swapped[1:], axis=0)
    slabs = [swapped[0], arrived]
    for step in range(1, cycle_size):
        slabs.append(lax.dynamic_slice_in_dim(gathered[step], member * width, width, axis=1))
        slabs.append(shifted(arrived, "cls", step))
    sums = pl.pallas_call(
        functools.partial(sums_kernel, team, cycle_size),
        out_shape=jax.ShapeDtypeStruct((proj_here, width), jnp.bfloat16),
        in_specs=[local] * (team + 2 * cycle_size),
        out_specs=local,
        cost_estimate=pl.CostEstimate(
            flops=2 * team * all_rows * proj_here * width,
            bytes_accessed=2 * (team * all_rows + proj_here) * width,
            transcendentals=0,
        ),
        compiler_params=grant(),
        name="sums",
    )(*weights, *slabs)
    blocks = sums.reshape(owners, proj_here // owners, width)
    pieces = lax.all_to_all(blocks, "img", 0, 0)
    pieces = pieces.reshape(owners // team, team, proj_here // owners, width)
    total = jnp.sum(pieces.astype(jnp.float32), axis=0)
    sum_rows = jnp.concatenate([total[place] for place in range(team)], axis=1)[:, :terms]
    return (sum_rows, evidence[:, 0])


def solution(mesh):
    in_specs = (
        P(("cls", "img"), None),
        P("cls", None),
        P(),
        P(),
        P(("cls", "img")),
        P(("cls", "img")),
    )
    out_specs = (P(("cls", "img"), None), P(("cls", "img")))
    return jax.shard_map(body, mesh=mesh, in_specs=in_specs, out_specs=out_specs, check_vma=False)
```

time: 49.8 us -> 53.1 us (1.066)
  matrix products: 9.02 us -> 0 us
  local copies, waits for them, and re-layouts: 1.28 us -> 9.2 us
  Pallas kernels: 0 us -> 7.22 us
  other arithmetic: 2.72 us -> 0.78 us
  waiting for transfers between devices: 21.6 us -> 20.5 us
    dot_general x6 -> x0, matrix products: 9.02 us -> none  [the longest x1 4.2 us: body(): jnp.dot(inverse, (proj_float * proj_float).T, precision=lax.Precision.HIG...]
    pallas_call x0 -> x5, Pallas kernels: none -> 7.22 us  [the longest x1 2.06 us: body(): pl.pallas_call(functools.partial(whiten_kernel, terms, tag_column, classe...]
    unnamed x5 -> x16, local copies, waits for them, and re-layouts: 0.01 us -> 6.73 us
    ppermute x5 -> x6, waiting for transfers between devices: 9.36 us -> 6.5 us  [crossed(): lax.ppermute(value, axis, [(place, place ^ flip) for place in range(count)])]
    dynamic_slice x1 -> x2, local copies, waits for them, and re-layouts: 0.2 us -> 1.8 us  [the longest x1 0.95 us: body(): lax.dynamic_slice_in_dim(gathered[step], member * width, width, axis=1)]
    eq x2 -> x0, other arithmetic: 1.32 us -> none  [the longest x1 0.66 us: body(): offsets[:, None] == jnp.arange(class_count, dtype=jnp.int32)[None, :]]
    ppermute x4 -> x3, waiting for transfers between devices: 0.01 us -> 1.23 us  [shifted(): lax.ppermute(value, axis, [(place, (place + step) % count) for place in r...]
    all_to_all x1, waiting for transfers between devices: 12.2 us -> 12.8 us  [body(): pieces = lax.all_to_all(blocks, 'img', 0, 0)]
  transfers between devices with their start and end apart: 10 -> 10, of which waited for: 4 -> 7; matrix products, arithmetic and copies ran while one was open for 19% -> 5% of each run, Pallas kernels for 0% -> 7%
where the time goes in v2:
time: 53.1 us; the launch traced here: 52.6 us
  waiting for transfers between devices  20.5 us (39%)
  starting transfers between devices  14.1 us (27%)
  local copies, waits for them, and re-layouts  9.2 us (17%)
  Pallas kernels  7.22 us (14%)
  other arithmetic  0.78 us (1%)
  between operations  0.74 us (1%)
    all_to_all x1, waiting for transfers between devices, body(): pieces = lax.all_to_all(blocks, 'img', 0, 0)  12.8 us
    ppermute x6, starting transfers between devices, crossed(): lax.ppermute(value, axis, [(place, place ^ flip) for place in range(count)])  7.61 us
    unnamed x16, local copies, waits for them, and re-layouts  6.73 us
    ppermute x6, waiting for transfers between devices, crossed(): lax.ppermute(value, axis, [(place, place ^ flip) for place in range(count)])  6.5 us
    all_to_all x1, starting transfers between devices, body(): pieces = lax.all_to_all(blocks, 'img', 0, 0)  5.82 us
    pallas_call x1, Pallas kernels, body(): pl.pallas_call(functools.partial(whiten_kernel, terms, tag_column, classe...  2.06 us
    pallas_call x1, Pallas kernels, body(): pl.pallas_call(functools.partial(score_kernel, tag_column, cycle_size), o...  1.95 us
    pallas_call x1, Pallas kernels, body(): pl.pallas_call(functools.partial(table_kernel, tag_column % LANES, per_cl...  1.7 us
  transfers between devices with their start and end apart: 10, of which 7 were waited for; matrix products, arithmetic and copies ran while one was open for 5% of the time, Pallas kernels for 7%

profile of v2, /device:TPU:0, one launch (start us, length us, event | category | flops | bytes accessed | tf_op | source)
XLA Modules:
  0.0 52.6 jit_solution(17286236107074702388)
XLA Ops:
  0.6 1.2 %copy-done.1 = f32[32,7200]{1,0:T(8,128)S(1)} copy-done((f32[32,7200]{1,0:T(8,128)S(1)}, f32[32,7200]{1,0:T(8,128)}, u32[]{:S(2)}) %copy-start.1) | copy-done | bytes 921624
  1.8 1.1 %copy-done.3 = bf16[56,7200]{1,0:T(8,128)(2,1)S(1)} copy-done((bf16[56,7200]{1,0:T(8,128)(2,1)S(1)}, bf16[56,7200]{1,0:T(8,128)(2,1)}, u32[]{:S(2)}) %copy-start.3) | copy-done | bytes 806424
  3.0 0.7 %copy-done.4 = s32[56]{0:T(128)S(1)} copy-done((s32[56]{0:T(128)S(1)}, s32[56]{0:T(128)}, u32[]{:S(2)}) %copy-start.4) | copy-done | bytes 248
  3.6 0.7 %copy-done.5 = s32[56]{0:T(128)S(1)} copy-done((s32[56]{0:T(128)S(1)}, s32[56]{0:T(128)}, u32[]{:S(2)}) %copy-start.5) | copy-done | bytes 248
  4.3 2.1 %whiten.1.refs_0_ = bf16[56,7680]{1,0:T(8,128)(2,1)S(1)} custom-call(s32[1,56]{1,0:T(1,128)S(1)} %bitcast.17, s32[1,56]{1,0:T(1,128)S(1)} %bitcast.18, bf16[56,7200]{1,0:T(8,128)(2,1)S(1)} %copy-done.3, f32[32,7200]{1,0:T(8,128)S(1)} %copy-done.1), custom_call_target="tpu_custom_call" | custom-call | flops 77414400 | bytes 2534400 | tf_op jit(solution)/shard_map/whiten/pallas_call | solution.py:191
  6.3 0.6 %collective-permute-start = (bf16[56,7680]{1,0:T(8,128)(2,1)S(1)}, bf16[56,7680]{1,0:T(8,128)(2,1)}, u32[]{:S(2)}, u32[]{:S(2)}) collective-permute-start(bf16[56,7680]{1,0:T(8,128)(2,1)S(1)} %whiten.1.refs_0_), channel_id=1, source_target_pairs={{0,16},{16,0},{1,17},{17,1},{2,18},{18,2},{3,19},{19,3},{4,20},{20... | collective-permute-start | bytes 2580488 | tf_op jit(solution)/shard_map/ppermute | solution.py:21
  6.9 0.9 %constant_dynamic-slice_fusion.1 = (bf16[56,1920]{1,0:T(8,128)(2,1)}, bf16[56,1920]{1,0:T(8,128)(2,1)}, bf16[56,1920]{1,0:T(8,128)(2,1)S(1)}, bf16[56,1920]{1,0:T(8,128)(2,1)S(1)}) fusion(bf16[56,7680]{1,0:T(8,128)(2,1)S(1)} %whiten.1.refs_0_, s32[]{:T(128)S(6)} %select_n.24, s32[]{:T(128)S(6)} %select_n.23, s32[]{:T(128)S(6)} %select_n.22, s32[]{:T(128)S(6)} %select_n.21), kind=kLoop, calls=%fused_computation.13 | loop fusion | bytes 1720336 | tf_op jit(solution)/shard_map/dynamic_slice | solution.py:228
  7.8 3.5 %collective-permute-start.7 = (bf16[56,1920]{1,0:T(8,128)(2,1)}, bf16[56,1920]{1,0:T(8,128)(2,1)S(1)}, u32[]{:S(2)}, u32[]{:S(2)}) collective-permute-start(bf16[56,1920]{1,0:T(8,128)(2,1)} %get-tuple-element.18), channel_id=1, source_target_pairs={{0,3},{1,2},{2,1},{3,0},{4,7},{5,6},{6,5},{7,4},{8,11},{9,10},{10,... | collective-permute-start | bytes 645128 | tf_op jit(solution)/shard_map/ppermute | solution.py:26
  11.8 1.2 %copy-done.2 = f32[32,7200]{1,0:T(8,128)S(1)} copy-done((f32[32,7200]{1,0:T(8,128)S(1)}, f32[32,7200]{1,0:T(8,128)}, u32[]{:S(2)}) %copy-start.2) | copy-done | bytes 921624
  13.0 1.7 %table.1.refs_3_ = f32[128,128]{1,0:T(8,128)S(1)} custom-call(s32[1]{0:T(128)} %bitcast.3.place_ref, f32[4]{0:T(128)S(1)} %copy-done.6, f32[32,7200]{1,0:T(8,128)S(1)} %copy-done.2, bf16[7200,128]{1,0:T(8,128)(2,1)S(1)} %bitcast.15), custom_call_target="tpu_custom_call" | custom-call | flops 235929600 | bytes 2764800 | tf_op jit(solution)/shard_map/table/pallas_call | solution.py:212
  14.7 2.0 %scores.1 = (f32[112,128]{1,0:T(8,128)S(1)}, f32[112,128]{1,0:T(8,128)S(1)}) custom-call(bf16[56,7680]{1,0:T(8,128)(2,1)S(1)} %whiten.1.refs_0_, bf16[56,7680]{1,0:T(8,128)(2,1)} %collective-permute-done.refs_1_, bf16[7200,128]{1,0:T(8,128)(2,1)S(1)} %bitcast.16, f32[128,128]{1,0:T(8,128)S(1)} %table.1.refs_3_), custom_call_target="tpu_custom_call" | custom-call | flops 206438400 | bytes 3456000 | tf_op jit(solution)/shard_map/scores/pallas_call | solution.py:233
  16.8 1.2 %collective-permute-done.1.refs_2_ = f32[112,128]{1,0:T(8,128)S(1)} collective-permute-done((f32[112,128]{1,0:T(8,128)S(1)}, f32[112,128]{1,0:T(8,128)S(1)}, u32[]{:S(2)}, u32[]{:S(2)}) %collective-permute-start.1) | collective-permute-done | bytes 57376 | tf_op jit(solution)/shard_map/ppermute | solution.py:21
  18.3 3.8 %collective-permute-done.6 = bf16[56,1920]{1,0:T(8,128)(2,1)} collective-permute-done((bf16[56,1920]{1,0:T(8,128)(2,1)}, bf16[56,1920]{1,0:T(8,128)(2,1)}, u32[]{:S(2)}, u32[]{:S(2)}) %collective-permute-start.6) | collective-permute-done | bytes 215072 | tf_op jit(solution)/shard_map/ppermute | solution.py:26
  22.4 0.9 %constant_dynamic-update-slice_fusion.2 = bf16[168,1920]{1,0:T(8,128)(2,1)S(1)} fusion(bf16[56,1920]{1,0:T(8,128)(2,1)} %collective-permute-done.5), kind=kLoop, calls=%fused_computation.11 | loop fusion | bytes 430080
  23.3 1.0 %constant_dynamic-update-slice_fusion.1 = bf16[168,1920]{1,0:T(8,128)(2,1)S(1)} fusion(bf16[168,1920]{1,0:T(8,128)(2,1)S(1)} %constant_dynamic-update-slice_fusion.2, bf16[56,1920]{1,0:T(8,128)(2,1)} %collective-permute-done.6), kind=kLoop, calls=%fused_computation.10 | loop fusion | bytes 430080
  24.4 1.5 %collective-permute-start.4 = (bf16[112,128]{1,0:T(8,128)(2,1)S(1)}, bf16[112,128]{1,0:T(8,128)(2,1)S(1)}, u32[]{:S(2)}, u32[]{:S(2)}) collective-permute-start(bf16[112,128]{1,0:T(8,128)(2,1)S(1)} %get-tuple-element.12.refs_0_), channel_id=1, source_target_pairs={{0,3},{1,2},{2,1},{3,0},{4,7},{5,6},{6,5},{7,4},{8,11},{9,10},{10,... | collective-permute-start | bytes 86024 | tf_op jit(solution)/shard_map/ppermute | solution.py:26
  25.9 1.5 %collective-permute-start.3 = (bf16[112,128]{1,0:T(8,128)(2,1)S(1)}, bf16[112,128]{1,0:T(8,128)(2,1)S(1)}, u32[]{:S(2)}, u32[]{:S(2)}) collective-permute-start(bf16[112,128]{1,0:T(8,128)(2,1)S(1)} %get-tuple-element.12.refs_0_), channel_id=1, source_target_pairs={{0,2},{1,3},{2,0},{3,1},{4,6},{5,7},{6,4},{7,5},{8,10},{9,11},{10,... | collective-permute-start | bytes 86024 | tf_op jit(solution)/shard_map/ppermute | solution.py:26
  28.0 0.9 %constant_dynamic-slice_fusion.refs_6_ = bf16[56,1920]{1,0:T(8,128)(2,1)S(1)} fusion(bf16[56,7680]{1,0:T(8,128)(2,1)} %collective-permute-done.refs_1_, s32[]{:T(128)S(6)} %select_n.21), kind=kLoop, calls=%fused_computation.12 | loop fusion | bytes 430084 | tf_op jit(solution)/shard_map/dynamic_slice | solution.py:267
  29.8 1.5 %collective-permute-done.2.refs_1_ = bf16[112,128]{1,0:T(8,128)(2,1)S(1)} collective-permute-done((bf16[112,128]{1,0:T(8,128)(2,1)S(1)}, bf16[112,128]{1,0:T(8,128)(2,1)S(1)}, u32[]{:S(2)}, u32[]{:S(2)}) %collective-permute-start.2) | collective-permute-done | bytes 28704 | tf_op jit(solution)/shard_map/ppermute | solution.py:26
  31.3 1.3 %sums.1 = bf16[128,1920]{1,0:T(8,128)(2,1)} custom-call(bf16[112,128]{1,0:T(8,128)(2,1)S(1)} %get-tuple-element.12.refs_0_, bf16[112,128]{1,0:T(8,128)(2,1)S(1)} %collective-permute-done.2.refs_1_, bf16[112,128]{1,0:T(8,128)(2,1)S(1)} %collective-permute-done.3.refs_2_, bf16[112,128]{1,0:T(8,128)(2,1)S(1)} %collective-permute-done.4.refs_3_, ...), custom_call_target="tpu_custom_call" | custom-call | flops 220200960 | bytes 2211840 | tf_op jit(solution)/shard_map/sums/pallas_call | solution.py:269
  32.5 5.8 %all-to-all-start = ((bf16[16,8,1920]{2,1,0:T(8,128)(2,1)}), bf16[16,8,1920]{2,1,0:T(8,128)(2,1)S(1)}, u32[]{:S(2)}, u32[]{:S(2)}) async-start(bf16[16,8,1920]{2,1,0:T(8,128)(2,1)} %bitcast.4), calls=%async_computation | async-start | bytes 983040 | tf_op jit(solution)/shard_map/all_to_all | solution.py:283
  38.4 0.6 %slice_reduce_fusion = f32[56]{0:T(128)} fusion(f32[56,128]{1,0:T(8,128)S(1)} %get-tuple-element.17), kind=kLoop, calls=%fused_computation.8 | loop fusion | bytes 448 | tf_op jit(solution)/shard_map/slice | solution.py:287
  39.0 12.8 %all-to-all-done = bf16[16,8,1920]{2,1,0:T(8,128)(2,1)S(1)} async-done(((bf16[16,8,1920]{2,1,0:T(8,128)(2,1)}), bf16[16,8,1920]{2,1,0:T(8,128)(2,1)S(1)}, u32[]{:S(2)}, u32[]{:S(2)}) %all-to-all-start) | async-done | bytes 491552 | tf_op jit(solution)/shard_map/all_to_all | solution.py:283
  51.9 0.7 %pad_maximum_fusion = f32[8,7200]{1,0:T(8,128)} fusion(f32[8,1920]{1,0:T(8,128)S(1)} %get-tuple-element.23, f32[8,1920]{1,0:T(8,128)S(1)} %get-tuple-element.24, f32[8,1920]{1,0:T(8,128)S(1)} %get-tuple-element.25, f32[8,1920]{1,0:T(8,128)S(1)} %get-tuple-element.22), kind=kLoop, calls=%fused_computation.1 | loop fusion | flops 172800 | bytes 476160 | tf_op jit(solution)/shard_map/concatenate | solution.py:286
  (24 shorter events, 2.8 us)
Async XLA Ops:
  0.6 1.2 %copy-start.1 = (f32[32,7200]{1,0:T(8,128)S(1)}, f32[32,7200]{1,0:T(8,128)}, u32[]{:S(2)}) copy-start(f32[32,7200]{1,0:T(8,128)} %noise_ref.3) | copy-start | bytes 2764804
  1.8 1.1 %copy-start.3 = (bf16[56,7200]{1,0:T(8,128)(2,1)S(1)}, bf16[56,7200]{1,0:T(8,128)(2,1)}, u32[]{:S(2)}) copy-start(bf16[56,7200]{1,0:T(8,128)(2,1)} %images_ref.1) | copy-start | bytes 2419204
  3.0 0.7 %copy-start.4 = (s32[56]{0:T(128)S(1)}, s32[56]{0:T(128)}, u32[]{:S(2)}) copy-start(s32[56]{0:T(128)} %param.10) | copy-start | bytes 676
  3.6 0.7 %copy-start.5 = (s32[56]{0:T(128)S(1)}, s32[56]{0:T(128)}, u32[]{:S(2)}) copy-start(s32[56]{0:T(128)} %param.11) | copy-start | bytes 676
  4.3 7.5 %copy-start = (bf16[128,7200]{0,1:T(8,128)(2,1)S(1)}, bf16[128,7200]{0,1:T(8,128)(2,1)}, u32[]{:S(2)}) copy-start(bf16[128,7200]{0,1:T(8,128)(2,1)} %param.7) | copy-start | bytes 5529604
  4.3 7.5 %copy-start.6 = (f32[4]{0:T(128)S(1)}, f32[4]{0:T(128)}, u32[]{:S(2)}) copy-start(f32[4]{0:T(128)} %prior_ref.1) | copy-start | bytes 52
  6.3 8.4 %collective-permute-start = (bf16[56,7680]{1,0:T(8,128)(2,1)S(1)}, bf16[56,7680]{1,0:T(8,128)(2,1)}, u32[]{:S(2)}, u32[]{:S(2)}) collective-permute-start(bf16[56,7680]{1,0:T(8,128)(2,1)S(1)} %whiten.1.refs_0_), channel_id=1, source_target_pairs={{0,16},{16,0},{1,17},{17,1},{2,18},{18,2},{3,19},{19,3},{4,20},{20... | collective-permute-start | bytes 2580488 | tf_op jit(solution)/shard_map/ppermute | solution.py:21
  7.8 10.5 %collective-permute-start.7 = (bf16[56,1920]{1,0:T(8,128)(2,1)}, bf16[56,1920]{1,0:T(8,128)(2,1)S(1)}, u32[]{:S(2)}, u32[]{:S(2)}) collective-permute-start(bf16[56,1920]{1,0:T(8,128)(2,1)} %get-tuple-element.18), channel_id=1, source_target_pairs={{0,3},{1,2},{2,1},{3,0},{4,7},{5,6},{6,5},{7,4},{8,11},{9,10},{10,... | collective-permute-start | bytes 645128 | tf_op jit(solution)/shard_map/ppermute | solution.py:26
  11.2 10.8 %collective-permute-start.6 = (bf16[56,1920]{1,0:T(8,128)(2,1)}, bf16[56,1920]{1,0:T(8,128)(2,1)}, u32[]{:S(2)}, u32[]{:S(2)}) collective-permute-start(bf16[56,1920]{1,0:T(8,128)(2,1)} %get-tuple-element.19), channel_id=1, source_target_pairs={{0,2},{1,3},{2,0},{3,1},{4,6},{5,7},{6,4},{7,5},{8,10},{9,11},{10,... | collective-permute-start | bytes 645128 | tf_op jit(solution)/shard_map/ppermute | solution.py:26
  11.8 10.6 %collective-permute-start.5 = (bf16[56,1920]{1,0:T(8,128)(2,1)S(1)}, bf16[56,1920]{1,0:T(8,128)(2,1)}, u32[]{:S(2)}, u32[]{:S(2)}) collective-permute-start(bf16[56,1920]{1,0:T(8,128)(2,1)S(1)} %get-tuple-element.20), channel_id=1, source_target_pairs={{0,1},{1,0},{2,3},{3,2},{4,5},{5,4},{6,7},{7,6},{8,9},{9,8},{10,11... | collective-permute-start | bytes 645128 | tf_op jit(solution)/shard_map/ppermute | solution.py:26
  11.8 1.2 %copy-start.2 = (f32[32,7200]{1,0:T(8,128)S(1)}, f32[32,7200]{1,0:T(8,128)}, u32[]{:S(2)}) copy-start(f32[32,7200]{1,0:T(8,128)} %noise_ref.3) | copy-start | bytes 2764804
  16.7 1.3 %collective-permute-start.1 = (f32[112,128]{1,0:T(8,128)S(1)}, f32[112,128]{1,0:T(8,128)S(1)}, u32[]{:S(2)}, u32[]{:S(2)}) collective-permute-start(f32[112,128]{1,0:T(8,128)S(1)} %get-tuple-element.11.refs_1_), channel_id=1, source_target_pairs={{0,16},{16,0},{1,17},{17,1},{2,18},{18,2},{3,19},{19,3},{4,20},{20... | collective-permute-start | bytes 172040 | tf_op jit(solution)/shard_map/ppermute | solution.py:21
  24.3 7.0 %collective-permute-start.8 = (bf16[168,1920]{1,0:T(8,128)(2,1)S(1)}, bf16[168,1920]{1,0:T(8,128)(2,1)S(1)}, u32[]{:S(2)}, u32[]{:S(2)}) collective-permute-start(bf16[168,1920]{1,0:T(8,128)(2,1)S(1)} %constant_dynamic-update-slice_fusion.refs_5_), channel_id=1, source_target_pairs={{0,16},{16,0},{1,17},{17,1},{2,18},{18,2},{3,19},{19,3},{4,20},{20... | collective-permute-start | bytes 1935368 | tf_op jit(solution)/shard_map/ppermute | solution.py:21
  24.4 4.8 %collective-permute-start.4 = (bf16[112,128]{1,0:T(8,128)(2,1)S(1)}, bf16[112,128]{1,0:T(8,128)(2,1)S(1)}, u32[]{:S(2)}, u32[]{:S(2)}) collective-permute-start(bf16[112,128]{1,0:T(8,128)(2,1)S(1)} %get-tuple-element.12.refs_0_), channel_id=1, source_target_pairs={{0,3},{1,2},{2,1},{3,0},{4,7},{5,6},{6,5},{7,4},{8,11},{9,10},{10,... | collective-permute-start | bytes 86024 | tf_op jit(solution)/shard_map/ppermute | solution.py:26
  25.9 3.9 %collective-permute-start.3 = (bf16[112,128]{1,0:T(8,128)(2,1)S(1)}, bf16[112,128]{1,0:T(8,128)(2,1)S(1)}, u32[]{:S(2)}, u32[]{:S(2)}) collective-permute-start(bf16[112,128]{1,0:T(8,128)(2,1)S(1)} %get-tuple-element.12.refs_0_), channel_id=1, source_target_pairs={{0,2},{1,3},{2,0},{3,1},{4,6},{5,7},{6,4},{7,5},{8,10},{9,11},{10,... | collective-permute-start | bytes 86024 | tf_op jit(solution)/shard_map/ppermute | solution.py:26
  27.4 3.9 %collective-permute-start.2 = (bf16[112,128]{1,0:T(8,128)(2,1)S(1)}, bf16[112,128]{1,0:T(8,128)(2,1)S(1)}, u32[]{:S(2)}, u32[]{:S(2)}) collective-permute-start(bf16[112,128]{1,0:T(8,128)(2,1)S(1)} %get-tuple-element.12.refs_0_), channel_id=1, source_target_pairs={{0,1},{1,0},{2,3},{3,2},{4,5},{5,4},{6,7},{7,6},{8,9},{9,8},{10,11... | collective-permute-start | bytes 86024 | tf_op jit(solution)/shard_map/ppermute | solution.py:26
  32.5 19.3 %all-to-all-start = ((bf16[16,8,1920]{2,1,0:T(8,128)(2,1)}), bf16[16,8,1920]{2,1,0:T(8,128)(2,1)S(1)}, u32[]{:S(2)}, u32[]{:S(2)}) async-start(bf16[16,8,1920]{2,1,0:T(8,128)(2,1)} %bitcast.4), calls=%async_computation | async-start | bytes 983040 | tf_op jit(solution)/shard_map/all_to_all | solution.py:283

commit v3 on v2

--- a/solution.py
+++ b/solution.py
@@ -6,6 +6,7 @@
 from jax.experimental import pallas as pl
 from jax.experimental.pallas import tpu as pltpu
 from jax.sharding import PartitionSpec as P
+
 
 LANES = 128
 PARTS = 3
@@ -43,63 +44,107 @@
     return lax.dot_general(left, right, (((0,), (0,)), ((), ())), preferred_element_type=jnp.float32)
 
 
-def column_of(shape, start):
-    return start + lax.broadcasted_iota(jnp.int32, shape, 1)
-
-
-def whiten_kernel(terms, tag_column, groups_ref, offsets_ref, images_ref, noise_ref, out_ref, *, classes):
-    step = pl.program_id(0)
-    rows, width = out_ref.shape
+def whiten_kernel(
+    team,
+    tag_column,
+    classes,
+    groups_hbm,
+    offsets_hbm,
+    images_hbm,
+    noise_hbm,
+    tall_hbm,
+    white_ref,
+    narrow_ref,
+    tall_ref,
+    *rest,
+):
+    part_refs = rest[:team]
+    groups_ref, offsets_ref, images_ref, noise_ref, *sems = rest[team:]
+    small_sems, image_sems, noise_sems, tall_sem = sems
+    rows, terms = images_ref.shape
+    width = white_ref.shape[1] // team
     group_count = noise_ref.shape[0]
+    spans = [(place * width, min(terms, (place + 1) * width)) for place in range(team)]
+    small = [
+        pltpu.make_async_copy(groups_hbm, groups_ref, small_sems.at[0]),
+        pltpu.make_async_copy(offsets_hbm, offsets_ref, small_sems.at[1]),
+    ]
+    for copy in small:
+        copy.start()
+    large = []
+    for place, (low, high) in enumerate(spans):
+        cut = pl.ds(low, high - low)
+        pair = (
+            pltpu.make_async_copy(noise_hbm.at[:, cut], noise_ref.at[:, cut], noise_sems.at[place]),
+            pltpu.make_async_copy(images_hbm.at[:, cut], images_ref.at[:, cut], image_sems.at[place]),
+        )
+        for copy in pair:
+            copy.start()
+        large.append(pair)
+    tall_copy = pltpu.make_async_copy(tall_hbm, tall_ref, tall_sem)
+    tall_copy.start()
 
     def hot(ids, count):
         places = lax.broadcasted_iota(jnp.int32, (count, rows), 0)
         return jnp.where(places == ids, 1.0, 0.0)
 
+    for copy in small:
+        copy.wait()
     group_hot = hot(groups_ref[...], group_count).astype(jnp.bfloat16)
-    pieces = split(1.0 / noise_ref[...], PARTS)
-    row_inverse = first_rows(
-        jnp.concatenate([group_hot] * PARTS, axis=0), jnp.concatenate(pieces, axis=0)
-    )
-    white = images_ref[...].astype(jnp.float32) * row_inverse
-    last = pl.num_programs(0) - 1
-
-    @pl.when(step != last)
-    def _():
-        out_ref[...] = white.astype(jnp.bfloat16)
-
-    @pl.when(step == last)
-    def _():
-        start = last * width
-        kept = jnp.where(column_of((rows, width), start) < terms, white, 0.0)
-        out_ref[...] = kept.astype(jnp.bfloat16)
-        tile = tag_column // LANES * LANES
-        for ids, count, shift in (
-            (groups_ref[...], group_count, tag_column - tile),
-            (offsets_ref[...], classes, tag_column - tile + group_count),
-        ):
-            tall = -(-count // 16) * 16
-            line = lax.broadcasted_iota(jnp.int32, (tall, LANES), 0)
-            lane = lax.broadcasted_iota(jnp.int32, (tall, LANES), 1)
-            spread = jnp.where(lane == line + shift, 1.0, 0.0).astype(jnp.bfloat16)
-            mark = first_rows(hot(ids, tall).astype(jnp.bfloat16), spread)
-            place = pl.ds(tile - start, LANES)
-            out_ref[:, place] = out_ref[:, place] + mark.astype(jnp.bfloat16)
-
-
-def table_kernel(shift, per_class, place_ref, prior_ref, noise_ref, tall_ref, out_ref):
-    group_count = noise_ref.shape[0]
+    chooser = jnp.concatenate([group_hot] * PARTS, axis=0)
+    member = lax.rem(lax.axis_index("img"), team)
+    for place, (low, high) in enumerate(spans):
+        noise_copy, image_copy = large[place]
+        noise_copy.wait()
+        pieces = split(1.0 / noise_ref[:, low:high], PARTS)
+        narrow_ref[:group_count, low:high] = pieces[0]
+        narrow_ref[group_count:, low:high] = pieces[1]
+        row_inverse = first_rows(chooser, jnp.concatenate(pieces, axis=0))
+        image_copy.wait()
+        white = images_ref[:, low:high].astype(jnp.float32) * row_inverse
+        missing = width - (high - low)
+        if missing:
+            white = jnp.concatenate([white, jnp.zeros((rows, missing), jnp.float32)], axis=1)
+            tile = tag_column // LANES * LANES
+            mark = jnp.zeros((rows, LANES), jnp.float32)
+            for ids, count, shift in (
+                (groups_ref[...], group_count, tag_column - tile),
+                (offsets_ref[...], classes, tag_column - tile + group_count),
+            ):
+                tall = -(-count // 16) * 16
+                line = lax.broadcasted_iota(jnp.int32, (tall, LANES), 0)
+                lane = lax.broadcasted_iota(jnp.int32, (tall, LANES), 1)
+                spread = jnp.where(lane == line + shift, 1.0, 0.0).astype(jnp.bfloat16)
+                mark = mark + first_rows(hot(ids, tall).astype(jnp.bfloat16), spread)
+            edge = tile - place * width
+            white = jnp.concatenate(
+                [white[:, :edge], white[:, edge : edge + LANES] + mark, white[:, edge + LANES :]],
+                axis=1,
+            )
+        white = white.astype(jnp.bfloat16)
+        white_ref[:, place * width : (place + 1) * width] = white
+        for flip, part_ref in enumerate(part_refs):
+
+            @pl.when(member == place ^ flip)
+            def _():
+                part_ref[...] = white
+
+    tall_copy.wait()
+
+
+def table_kernel(shift, per_class, prior_ref, narrow_ref, tall_ref, out_ref):
+    group_count = narrow_ref.shape[0] // 2
     proj_here = tall_ref.shape[1]
     class_count = prior_ref.shape[0]
     tall = tall_ref[...].astype(jnp.float32)
     high, low = split(tall * tall, 2)
-    narrow = jnp.concatenate(split(1.0 / noise_ref[...], 2), axis=0)
+    narrow = narrow_ref[...]
     both = jnp.dot(narrow, high, preferred_element_type=jnp.float32) + jnp.dot(
         narrow, low, preferred_element_type=jnp.float32
     )
     out_ref[...] = jnp.zeros_like(out_ref)
     out_ref[pl.ds(shift, group_count), :] = -0.5 * (both[:group_count] + both[group_count:])
-    index = place_ref[0] * proj_here + lax.broadcasted_iota(jnp.int32, (1, proj_here), 1)
+    index = lax.axis_index("cls") * proj_here + lax.broadcasted_iota(jnp.int32, (1, proj_here), 1)
     class_of = jnp.zeros_like(index)
     for bound in range(1, class_count):
         class_of = class_of + jnp.where(index >= bound * per_class, 1, 0)
@@ -115,7 +160,7 @@
 def score_kernel(tag_column, count, *refs):
     white_refs = refs[:count]
     tall_ref, table_ref, scores_ref, stats_ref = refs[count:]
-    terms, proj_here = tall_ref.shape
+    terms, _ = tall_ref.shape
     tile = tag_column // LANES * LANES
     rows = jnp.concatenate([ref[:, :tile] for ref in white_refs], axis=0)
     marks = jnp.concatenate([ref[:, tile : tile + LANES] for ref in white_refs], axis=0)
@@ -156,12 +201,19 @@
 def sums_kernel(team, count, *refs):
     weight_refs, slab_refs, out_ref = refs[:team], refs[team:-1], refs[-1]
     rows_here = weight_refs[0].shape[0] // count
+    width = out_ref.shape[1]
     weights = [
         ref[pl.ds(place * rows_here, rows_here), :]
         for place in range(count)
         for ref in weight_refs
     ]
-    slabs = [ref[...] for ref in slab_refs]
+    member = lax.rem(lax.axis_index("img"), team)
+    slabs = []
+    for place, ref in enumerate(slab_refs):
+        if place and place % team == 0:
+            slabs.append(ref[:, pl.ds(pl.multiple_of(member * width, LANES), width)])
+        else:
+            slabs.append(ref[...])
     out_ref[...] = first_rows(
         jnp.concatenate(weights, axis=0), jnp.concatenate(slabs, axis=0)
     ).astype(out_ref.dtype)
@@ -171,10 +223,8 @@
     rows_here, terms = images.shape
     proj_here = projections.shape[0]
     cycle_size = lax.axis_size("cls")
-    cycle_place = lax.axis_index("cls")
     owners = lax.axis_size("img")
     team = group_of(owners)
-    member = lax.axis_index("img") % team
     group_count = noise_power.shape[0]
     class_count = class_logprior.shape[0]
     tags = group_count + class_count
@@ -182,37 +232,56 @@
     width = -(-(tag_column + tags) // (LANES * team)) * LANES
     per_class = proj_here * cycle_size // class_count
     all_rows = cycle_size * rows_here
-    columns = functools.partial(pl.BlockSpec, index_map=lambda j: (0, j))
-    still = functools.partial(pl.BlockSpec, index_map=lambda j: (0, 0))
     grant = functools.partial(pltpu.CompilerParams, vmem_limit_bytes=GRANT)
     scalars = pl.BlockSpec(memory_space=pltpu.SMEM)
     local = pl.BlockSpec(memory_space=pltpu.VMEM)
 
-    whitened = pl.pallas_call(
-        functools.partial(whiten_kernel, terms, tag_column, classes=class_count),
-        out_shape=jax.ShapeDtypeStruct((rows_here, team * width), jnp.bfloat16),
-        grid=(team,),
-        in_specs=[
-            still((1, rows_here)),
-            still((1, rows_here)),
-            columns((rows_here, width)),
-            columns((group_count, width)),
+    remote = pl.BlockSpec(memory_space=pltpu.HBM)
+
+    whitened, narrow, tall, *parts = pl.pallas_call(
+        functools.partial(whiten_kernel, team, tag_column, class_count),
+        out_shape=(
+            jax.ShapeDtypeStruct((rows_here, team * width), jnp.bfloat16),
+            jax.ShapeDtypeStruct((2 * group_count, terms), jnp.bfloat16),
+            jax.ShapeDtypeStruct((terms, proj_here), jnp.bfloat16),
+        )
+        + (jax.ShapeDtypeStruct((rows_here, width), jnp.bfloat16),) * team,
+        in_specs=[remote] * 5,
+        out_specs=(local,) * (3 + team),
+        scratch_shapes=[
+            pltpu.VMEM((1, rows_here), jnp.int32),
+            pltpu.VMEM((1, rows_here), jnp.int32),
+            pltpu.VMEM((rows_here, terms), jnp.bfloat16),
+            pltpu.VMEM((group_count, terms), jnp.float32),
+            pltpu.SemaphoreType.DMA((2,)),
+            pltpu.SemaphoreType.DMA((team,)),
+            pltpu.SemaphoreType.DMA((team,)),
+            pltpu.SemaphoreType.DMA,
         ],
-        out_specs=columns((rows_here, width)),
-        compiler_params=grant(dimension_semantics=("arbitrary",)),
+        compiler_params=grant(),
         cost_estimate=pl.CostEstimate(
             flops=2 * rows_here * PARTS * group_count * terms,
             bytes_accessed=4 * rows_here * terms + 4 * group_count * terms,
             transcendentals=0,
         ),
         name="whiten",
-    )(groups.reshape(1, rows_here), offsets.reshape(1, rows_here), images, noise_power)
-
-    tall = projections.T
+    )(
+        *(
+            pltpu.with_memory_space_constraint(value, pltpu.HBM)
+            for value in (
+                groups.reshape(1, rows_here),
+                offsets.reshape(1, rows_here),
+                images,
+                noise_power,
+                projections.T,
+            )
+        ),
+    )
+
     table = pl.pallas_call(
         functools.partial(table_kernel, tag_column % LANES, per_class),
         out_shape=jax.ShapeDtypeStruct((LANES, proj_here), jnp.float32),
-        in_specs=[scalars, scalars, local, local],
+        in_specs=[scalars, local, local],
         out_specs=local,
         cost_estimate=pl.CostEstimate(
             flops=8 * proj_here * group_count * terms,
@@ -221,13 +290,9 @@
         ),
         compiler_params=grant(),
         name="table",
-    )(cycle_place.reshape(1), class_logprior, noise_power, tall)
+    )(class_logprior, narrow, tall)
 
     gathered = gathered_from(whitened, "cls")
-    parts = [
-        lax.dynamic_slice_in_dim(whitened, (member ^ flip) * width, width, axis=1)
-        for flip in range(team)
-    ]
     swapped = [parts[0]] + [crossed(parts[flip], "img", flip) for flip in range(1, team)]
 
     scores, stats = pl.pallas_call(
@@ -259,17 +324,18 @@
         name="posterior",
     )(scores, *gathered_from(stats, "cls"))
 
-    weights = [posterior] + [crossed(posterior, "img", flip) for flip in range(1, team)]
-    swapped, _ = lax.optimization_barrier((swapped, posterior))
-    arrived = jnp.concatenate(swapped[1:], axis=0)
-    slabs = [swapped[0], arrived]
+    weights = [posterior]
+    for flip in range(1, team):
+        weights.append(crossed(posterior, "img", flip))
+    slabs = list(swapped)
     for step in range(1, cycle_size):
-        slabs.append(lax.dynamic_slice_in_dim(gathered[step], member * width, width, axis=1))
-        slabs.append(shifted(arrived, "cls", step))
+        slabs.append(gathered[step])
+        for flip in range(1, team):
+            slabs.append(shifted(swapped[flip], "cls", step))
     sums = pl.pallas_call(
         functools.partial(sums_kernel, team, cycle_size),
         out_shape=jax.ShapeDtypeStruct((proj_here, width), jnp.bfloat16),
-        in_specs=[local] * (team + 2 * cycle_size),
+        in_specs=[local] * (team + team * cycle_size),
         out_specs=local,
         cost_estimate=pl.CostEstimate(
             flops=2 * team * all_rows * proj_here * width,

time: 53.1 us -> 51 us (0.960)
  local copies, waits for them, and re-layouts: 9.2 us -> 0.65 us
  waiting for transfers between devices: 20.5 us -> 27.7 us
    ppermute x6, waiting for transfers between devices: 6.5 us -> 14 us  [crossed(): lax.ppermute(value, axis, [(place, place ^ flip) for place in range(count)])]
    unnamed x16 -> x2, local copies, waits for them, and re-layouts: 6.73 us -> 0.01 us
    dynamic_slice x2 -> x0, local copies, waits for them, and re-layouts: 1.8 us -> none  [the longest x1 0.95 us: body(): lax.dynamic_slice_in_dim(gathered[step], member * width, width, axis=1)]
    pallas_call x1, Pallas kernels: 1.95 us -> 0.79 us  [body(): pl.pallas_call(functools.partial(score_kernel, tag_column, cycle_size), o...]
    pallas_call x1, Pallas kernels: 2.06 us -> 2.64 us  [body(): pl.pallas_call(functools.partial(whiten_kernel, team, tag_column, class_c...]
    ppermute x3 -> x5, starting transfers between devices: 0.7 us -> 1.16 us  [shifted(): lax.ppermute(value, axis, [(place, (place + step) % count) for place in r...]
    ppermute x3 -> x5, waiting for transfers between devices: 1.23 us -> 1.24 us  [shifted(): lax.ppermute(value, axis, [(place, (place + step) % count) for place in r...]
  transfers between devices with their start and end apart: 10 -> 12, of which waited for: 7 -> 7; matrix products, arithmetic and copies ran while one was open for 5% -> 1% of each run, Pallas kernels for 7% -> 6%
where the time goes in v3:
time: 51 us; the launch traced here: 50.8 us
  waiting for transfers between devices  27.7 us (54%)
  starting transfers between devices  14.2 us (28%)
  Pallas kernels  6.72 us (13%)
  other arithmetic  0.78 us (2%)
  between operations  0.7 us (1%)
  local copies, waits for them, and re-layouts  0.65 us (1%)
    ppermute x6, waiting for transfers between devices, crossed(): lax.ppermute(value, axis, [(place, place ^ flip) for place in range(count)])  14 us
    all_to_all x1, waiting for transfers between devices, body(): pieces = lax.all_to_all(blocks, 'img', 0, 0)  12.5 us
    ppermute x6, starting transfers between devices, crossed(): lax.ppermute(value, axis, [(place, place ^ flip) for place in range(count)])  7.7 us
    all_to_all x1, starting transfers between devices, body(): pieces = lax.all_to_all(blocks, 'img', 0, 0)  5.38 us
    pallas_call x1, Pallas kernels, body(): pl.pallas_call(functools.partial(whiten_kernel, team, tag_column, class_c...  2.64 us
    pallas_call x1, Pallas kernels, body(): pl.pallas_call(functools.partial(table_kernel, tag_column % LANES, per_cl...  1.76 us
    pallas_call x1, Pallas kernels, body(): pl.pallas_call(functools.partial(sums_kernel, team, cycle_size), out_shap...  1.27 us
    ppermute x5, waiting for transfers between devices, shifted(): lax.ppermute(value, axis, [(place, (place + step) % count) for place in r...  1.24 us
  transfers between devices with their start and end apart: 12, of which 7 were waited for; matrix products, arithmetic and copies ran while one was open for 1% of the time, Pallas kernels for 6%

profile of v3, /device:TPU:0, one launch (start us, length us, event | category | flops | bytes accessed | tf_op | source)
XLA Modules:
  0.0 50.8 jit_solution(10688306267545556313)
XLA Ops:
  0.6 2.6 %whiten.1 = (bf16[56,7680]{1,0:T(8,128)(2,1)S(1)}, bf16[64,7200]{1,0:T(8,128)(2,1)S(1)}, bf16[7200,128]{1,0:T(8,128)(2,1)S(1)}, bf16[56,1920]{1,0:T(8,128)(2,1)S...) custom-call(s32[1,56]{1,0:T(1,128)} %bitcast.16, s32[1,56]{1,0:T(1,128)} %bitcast.17, ...), custom_call_target="tpu_custom_call" | custom-call | flops 77414400 | bytes 2534400 | tf_op jit(solution)/shard_map/whiten/pallas_call | solution.py:241
  3.3 0.6 %collective-permute-start = (bf16[56,7680]{1,0:T(8,128)(2,1)S(1)}, bf16[56,7680]{1,0:T(8,128)(2,1)S(1)}, u32[]{:S(2)}, u32[]{:S(2)}) collective-permute-start(bf16[56,7680]{1,0:T(8,128)(2,1)S(1)} %get-tuple-element.13.refs_0_), channel_id=1, source_target_pairs={{0,16},{16,0},{1,17},{17,1},{2,18},{18,2},{3,19},{19,3},{4,20},{20... | collective-permute-start | bytes 2580488 | tf_op jit(solution)/shard_map/ppermute | solution.py:22
  3.9 3.5 %collective-permute-start.7 = (bf16[56,1920]{1,0:T(8,128)(2,1)S(1)}, bf16[56,1920]{1,0:T(8,128)(2,1)S(1)}, u32[]{:S(2)}, u32[]{:S(2)}) collective-permute-start(bf16[56,1920]{1,0:T(8,128)(2,1)S(1)} %get-tuple-element.22), channel_id=1, source_target_pairs={{0,3},{1,2},{2,1},{3,0},{4,7},{5,6},{6,5},{7,4},{8,11},{9,10},{10,... | collective-permute-start | bytes 645128 | tf_op jit(solution)/shard_map/ppermute | solution.py:27
  7.4 0.5 %collective-permute-start.5 = (bf16[56,1920]{1,0:T(8,128)(2,1)S(1)}, bf16[56,1920]{1,0:T(8,128)(2,1)S(1)}, u32[]{:S(2)}, u32[]{:S(2)}) collective-permute-start(bf16[56,1920]{1,0:T(8,128)(2,1)S(1)} %get-tuple-element.20), channel_id=1, source_target_pairs={{0,1},{1,0},{2,3},{3,2},{4,5},{5,4},{6,7},{7,6},{8,9},{9,8},{10,11... | collective-permute-start | bytes 645128 | tf_op jit(solution)/shard_map/ppermute | solution.py:27
  7.9 0.1 collective-permute-start.6
  8.0 5.5 %collective-permute-done.7.refs_7_ = bf16[56,1920]{1,0:T(8,128)(2,1)S(1)} collective-permute-done((bf16[56,1920]{1,0:T(8,128)(2,1)S(1)}, bf16[56,1920]{1,0:T(8,128)(2,1)S(1)}, u32[]{:S(2)}, u32[]{:S(2)}) %collective-permute-start.7) | collective-permute-done | bytes 215072 | tf_op jit(solution)/shard_map/ppermute | solution.py:27
  13.6 4.6 %collective-permute-done.5.refs_5_ = bf16[56,1920]{1,0:T(8,128)(2,1)S(1)} collective-permute-done((bf16[56,1920]{1,0:T(8,128)(2,1)S(1)}, bf16[56,1920]{1,0:T(8,128)(2,1)S(1)}, u32[]{:S(2)}, u32[]{:S(2)}) %collective-permute-start.5) | collective-permute-done | bytes 215072 | tf_op jit(solution)/shard_map/ppermute | solution.py:27
  18.2 0.5 collective-permute-start.9
  18.7 1.8 %table.1.refs_3_ = f32[128,128]{1,0:T(8,128)S(1)} custom-call(f32[4]{0:T(128)S(1)} %copy-done, bf16[64,7200]{1,0:T(8,128)(2,1)S(1)} %get-tuple-element.15.narrow_ref, bf16[7200,128]{1,0:T(8,128)(2,1)S(1)} %get-tuple-element.14.tall_ref.refs_2_), custom_call_target="tpu_custom_call" | custom-call | flops 235929600 | bytes 2764800 | tf_op jit(solution)/shard_map/table/pallas_call | solution.py:281
  20.5 0.8 %scores.1 = (f32[112,128]{1,0:T(8,128)S(1)}, f32[112,128]{1,0:T(8,128)S(1)}) custom-call(bf16[56,7680]{1,0:T(8,128)(2,1)S(1)} %get-tuple-element.13.refs_0_, bf16[56,7680]{1,0:T(8,128)(2,1)S(1)} %collective-permute-done.refs_1_.refs_8_, bf16[7200,128]{1,0:T(8,128)(2,1)S(1)} %get-tuple-element.14.tall_ref.refs_2_, f32[128,128]{1,0:T(8,128)S(1)} %table.1.refs_3_), custom_call_target="tpu_custom_call" | custom-call | flops 206438400 | bytes 3456000 | tf_op jit(solution)/shard_map/scores/pallas_call | solution.py:298
  21.2 0.1 collective-permute-start.1
  21.3 1.2 %collective-permute-done.1.refs_2_ = f32[112,128]{1,0:T(8,128)S(1)} collective-permute-done((f32[112,128]{1,0:T(8,128)S(1)}, f32[112,128]{1,0:T(8,128)S(1)}, u32[]{:S(2)}, u32[]{:S(2)}) %collective-permute-start.1) | collective-permute-done | bytes 57376 | tf_op jit(solution)/shard_map/ppermute | solution.py:22
  22.6 0.3 posterior.1
  22.8 1.6 %collective-permute-start.2 = (bf16[112,128]{1,0:T(8,128)(2,1)S(1)}, bf16[112,128]{1,0:T(8,128)(2,1)S(1)}, u32[]{:S(2)}, u32[]{:S(2)}) collective-permute-start(bf16[112,128]{1,0:T(8,128)(2,1)S(1)} %get-tuple-element.18.refs_0_), channel_id=1, source_target_pairs={{0,1},{1,0},{2,3},{3,2},{4,5},{5,4},{6,7},{7,6},{8,9},{9,8},{10,11... | collective-permute-start | bytes 86024 | tf_op jit(solution)/shard_map/ppermute | solution.py:27
  24.4 1.1 %collective-permute-start.3 = (bf16[112,128]{1,0:T(8,128)(2,1)S(1)}, bf16[112,128]{1,0:T(8,128)(2,1)S(1)}, u32[]{:S(2)}, u32[]{:S(2)}) collective-permute-start(bf16[112,128]{1,0:T(8,128)(2,1)S(1)} %get-tuple-element.18.refs_0_), channel_id=1, source_target_pairs={{0,2},{1,3},{2,0},{3,1},{4,6},{5,7},{6,4},{7,5},{8,10},{9,11},{10,... | collective-permute-start | bytes 86024 | tf_op jit(solution)/shard_map/ppermute | solution.py:27
  25.4 0.9 %collective-permute-start.4 = (bf16[112,128]{1,0:T(8,128)(2,1)S(1)}, bf16[112,128]{1,0:T(8,128)(2,1)S(1)}, u32[]{:S(2)}, u32[]{:S(2)}) collective-permute-start(bf16[112,128]{1,0:T(8,128)(2,1)S(1)} %get-tuple-element.18.refs_0_), channel_id=1, source_target_pairs={{0,3},{1,2},{2,1},{3,0},{4,7},{5,6},{6,5},{7,4},{8,11},{9,10},{10,... | collective-permute-start | bytes 86024 | tf_op jit(solution)/shard_map/ppermute | solution.py:27
  26.4 0.4 collective-permute-done.2.refs_1_
  26.8 1.5 %collective-permute-done.3.refs_2_ = bf16[112,128]{1,0:T(8,128)(2,1)S(1)} collective-permute-done((bf16[112,128]{1,0:T(8,128)(2,1)S(1)}, bf16[112,128]{1,0:T(8,128)(2,1)S(1)}, u32[]{:S(2)}, u32[]{:S(2)}) %collective-permute-start.3) | collective-permute-done | bytes 28704 | tf_op jit(solution)/shard_map/ppermute | solution.py:27
  28.2 2.0 %collective-permute-done.4.refs_3_ = bf16[112,128]{1,0:T(8,128)(2,1)S(1)} collective-permute-done((bf16[112,128]{1,0:T(8,128)(2,1)S(1)}, bf16[112,128]{1,0:T(8,128)(2,1)S(1)}, u32[]{:S(2)}, u32[]{:S(2)}) %collective-permute-start.4) | collective-permute-done | bytes 28704 | tf_op jit(solution)/shard_map/ppermute | solution.py:27
  30.2 1.3 %sums.1 = bf16[128,1920]{1,0:T(8,128)(2,1)} custom-call(bf16[112,128]{1,0:T(8,128)(2,1)S(1)} %get-tuple-element.18.refs_0_, bf16[112,128]{1,0:T(8,128)(2,1)S(1)} %collective-permute-done.2.refs_1_, bf16[112,128]{1,0:T(8,128)(2,1)S(1)} %collective-permute-done.3.refs_2_, bf16[112,128]{1,0:T(8,128)(2,1)S(1)} %collective-permute-done.4.refs_3_, ...), custom_call_target="tpu_custom_call" | custom-call | flops 220200960 | bytes 2211840 | tf_op jit(solution)/shard_map/sums/pallas_call | solution.py:335
  31.5 5.4 %all-to-all-start = ((bf16[16,8,1920]{2,1,0:T(8,128)(2,1)}), bf16[16,8,1920]{2,1,0:T(8,128)(2,1)S(1)}, u32[]{:S(2)}, u32[]{:S(2)}) async-start(bf16[16,8,1920]{2,1,0:T(8,128)(2,1)} %bitcast.3), calls=%async_computation | async-start | bytes 983040 | tf_op jit(solution)/shard_map/all_to_all | solution.py:349
  36.9 0.6 %slice_reduce_fusion = f32[56]{0:T(128)} fusion(f32[56,128]{1,0:T(8,128)S(1)} %get-tuple-element.23), kind=kLoop, calls=%fused_computation.8 | loop fusion | bytes 448 | tf_op jit(solution)/shard_map/slice | solution.py:353
  37.5 12.5 %all-to-all-done = bf16[16,8,1920]{2,1,0:T(8,128)(2,1)S(1)} async-done(((bf16[16,8,1920]{2,1,0:T(8,128)(2,1)}), bf16[16,8,1920]{2,1,0:T(8,128)(2,1)S(1)}, u32[]{:S(2)}, u32[]{:S(2)}) %all-to-all-start) | async-done | bytes 491552 | tf_op jit(solution)/shard_map/all_to_all | solution.py:349
  50.1 0.7 %pad_maximum_fusion = f32[8,7200]{1,0:T(8,128)} fusion(f32[8,1920]{1,0:T(8,128)S(1)} %get-tuple-element.25, f32[8,1920]{1,0:T(8,128)S(1)} %get-tuple-element.26, f32[8,1920]{1,0:T(8,128)S(1)} %get-tuple-element.27, f32[8,1920]{1,0:T(8,128)S(1)} %get-tuple-element.24), kind=kLoop, calls=%fused_computation.1 | loop fusion | flops 172800 | bytes 476160 | tf_op jit(solution)/shard_map/concatenate | solution.py:352
  (11 shorter events, 0.1 us)
Async XLA Ops:
  0.6 18.0 %copy-start = (f32[4]{0:T(128)S(1)}, f32[4]{0:T(128)}, u32[]{:S(2)}) copy-start(f32[4]{0:T(128)} %prior_ref.1) | copy-start | bytes 52
  3.3 17.2 %collective-permute-start = (bf16[56,7680]{1,0:T(8,128)(2,1)S(1)}, bf16[56,7680]{1,0:T(8,128)(2,1)S(1)}, u32[]{:S(2)}, u32[]{:S(2)}) collective-permute-start(bf16[56,7680]{1,0:T(8,128)(2,1)S(1)} %get-tuple-element.13.refs_0_), channel_id=1, source_target_pairs={{0,16},{16,0},{1,17},{17,1},{2,18},{18,2},{3,19},{19,3},{4,20},{20... | collective-permute-start | bytes 2580488 | tf_op jit(solution)/shard_map/ppermute | solution.py:22
  3.9 9.7 %collective-permute-start.7 = (bf16[56,1920]{1,0:T(8,128)(2,1)S(1)}, bf16[56,1920]{1,0:T(8,128)(2,1)S(1)}, u32[]{:S(2)}, u32[]{:S(2)}) collective-permute-start(bf16[56,1920]{1,0:T(8,128)(2,1)S(1)} %get-tuple-element.22), channel_id=1, source_target_pairs={{0,3},{1,2},{2,1},{3,0},{4,7},{5,6},{6,5},{7,4},{8,11},{9,10},{10,... | collective-permute-start | bytes 645128 | tf_op jit(solution)/shard_map/ppermute | solution.py:27
  7.4 10.8 %collective-permute-start.5 = (bf16[56,1920]{1,0:T(8,128)(2,1)S(1)}, bf16[56,1920]{1,0:T(8,128)(2,1)S(1)}, u32[]{:S(2)}, u32[]{:S(2)}) collective-permute-start(bf16[56,1920]{1,0:T(8,128)(2,1)S(1)} %get-tuple-element.20), channel_id=1, source_target_pairs={{0,1},{1,0},{2,3},{3,2},{4,5},{5,4},{6,7},{7,6},{8,9},{9,8},{10,11... | collective-permute-start | bytes 645128 | tf_op jit(solution)/shard_map/ppermute | solution.py:27
  7.9 10.3 %collective-permute-start.6 = (bf16[56,1920]{1,0:T(8,128)(2,1)S(1)}, bf16[56,1920]{1,0:T(8,128)(2,1)S(1)}, u32[]{:S(2)}, u32[]{:S(2)}) collective-permute-start(bf16[56,1920]{1,0:T(8,128)(2,1)S(1)} %get-tuple-element.21), channel_id=1, source_target_pairs={{0,2},{1,3},{2,0},{3,1},{4,6},{5,7},{6,4},{7,5},{8,10},{9,11},{10,... | collective-permute-start | bytes 645128 | tf_op jit(solution)/shard_map/ppermute | solution.py:27
  13.6 11.9 %collective-permute-start.10 = (bf16[56,1920]{1,0:T(8,128)(2,1)S(1)}, bf16[56,1920]{1,0:T(8,128)(2,1)S(1)}, u32[]{:S(2)}, u32[]{:S(2)}) collective-permute-start(bf16[56,1920]{1,0:T(8,128)(2,1)S(1)} %collective-permute-done.7.refs_7_), channel_id=1, source_target_pairs={{0,16},{16,0},{1,17},{17,1},{2,18},{18,2},{3,19},{19,3},{4,20},{20... | collective-permute-start | bytes 645128 | tf_op jit(solution)/shard_map/ppermute | solution.py:22
  18.2 8.2 %collective-permute-start.8 = (bf16[56,1920]{1,0:T(8,128)(2,1)S(1)}, bf16[56,1920]{1,0:T(8,128)(2,1)S(1)}, u32[]{:S(2)}, u32[]{:S(2)}) collective-permute-start(bf16[56,1920]{1,0:T(8,128)(2,1)S(1)} %collective-permute-done.5.refs_5_), channel_id=1, source_target_pairs={{0,16},{16,0},{1,17},{17,1},{2,18},{18,2},{3,19},{19,3},{4,20},{20... | collective-permute-start | bytes 645128 | tf_op jit(solution)/shard_map/ppermute | solution.py:22
  18.2 8.2 %collective-permute-start.9 = (bf16[56,1920]{1,0:T(8,128)(2,1)S(1)}, bf16[56,1920]{1,0:T(8,128)(2,1)S(1)}, u32[]{:S(2)}, u32[]{:S(2)}) collective-permute-start(bf16[56,1920]{1,0:T(8,128)(2,1)S(1)} %collective-permute-done.6.refs_6_), channel_id=1, source_target_pairs={{0,16},{16,0},{1,17},{17,1},{2,18},{18,2},{3,19},{19,3},{4,20},{20... | collective-permute-start | bytes 645128 | tf_op jit(solution)/shard_map/ppermute | solution.py:22
  21.2 1.3 %collective-permute-start.1 = (f32[112,128]{1,0:T(8,128)S(1)}, f32[112,128]{1,0:T(8,128)S(1)}, u32[]{:S(2)}, u32[]{:S(2)}) collective-permute-start(f32[112,128]{1,0:T(8,128)S(1)} %get-tuple-element.17.refs_1_), channel_id=1, source_target_pairs={{0,16},{16,0},{1,17},{17,1},{2,18},{18,2},{3,19},{19,3},{4,20},{20... | collective-permute-start | bytes 172040 | tf_op jit(solution)/shard_map/ppermute | solution.py:22
  22.8 3.9 %collective-permute-start.2 = (bf16[112,128]{1,0:T(8,128)(2,1)S(1)}, bf16[112,128]{1,0:T(8,128)(2,1)S(1)}, u32[]{:S(2)}, u32[]{:S(2)}) collective-permute-start(bf16[112,128]{1,0:T(8,128)(2,1)S(1)} %get-tuple-element.18.refs_0_), channel_id=1, source_target_pairs={{0,1},{1,0},{2,3},{3,2},{4,5},{5,4},{6,7},{7,6},{8,9},{9,8},{10,11... | collective-permute-start | bytes 86024 | tf_op jit(solution)/shard_map/ppermute | solution.py:27
  24.4 3.9 %collective-permute-start.3 = (bf16[112,128]{1,0:T(8,128)(2,1)S(1)}, bf16[112,128]{1,0:T(8,128)(2,1)S(1)}, u32[]{:S(2)}, u32[]{:S(2)}) collective-permute-start(bf16[112,128]{1,0:T(8,128)(2,1)S(1)} %get-tuple-element.18.refs_0_), channel_id=1, source_target_pairs={{0,2},{1,3},{2,0},{3,1},{4,6},{5,7},{6,4},{7,5},{8,10},{9,11},{10,... | collective-permute-start | bytes 86024 | tf_op jit(solution)/shard_map/ppermute | solution.py:27
  25.4 4.8 %collective-permute-start.4 = (bf16[112,128]{1,0:T(8,128)(2,1)S(1)}, bf16[112,128]{1,0:T(8,128)(2,1)S(1)}, u32[]{:S(2)}, u32[]{:S(2)}) collective-permute-start(bf16[112,128]{1,0:T(8,128)(2,1)S(1)} %get-tuple-element.18.refs_0_), channel_id=1, source_target_pairs={{0,3},{1,2},{2,1},{3,0},{4,7},{5,6},{6,5},{7,4},{8,11},{9,10},{10,... | collective-permute-start | bytes 86024 | tf_op jit(solution)/shard_map/ppermute | solution.py:27
  31.5 18.5 %all-to-all-start = ((bf16[16,8,1920]{2,1,0:T(8,128)(2,1)}), bf16[16,8,1920]{2,1,0:T(8,128)(2,1)S(1)}, u32[]{:S(2)}, u32[]{:S(2)}) async-start(bf16[16,8,1920]{2,1,0:T(8,128)(2,1)} %bitcast.3), calls=%async_computation | async-start | bytes 983040 | tf_op jit(solution)/shard_map/all_to_all | solution.py:349
